TPU v7x, 512 devices: a whole 4x8x8 slice. The times are simulated.
512 devices in a mesh: row: 16 (over y, core), col: 32 (over z, x).
Axes of the slice: x: 4, y: 8, z: 8, core: 2. Of those that a mesh axis runs over, the one named last changes fastest.
Arguments:
- feat: bfloat16 [64, 512, 512], P('row', 'col'), may hold values from -6 to 6
- ln_gain: float32 [512], replicated, may hold values from 0.1 to 1.9
- in_weight: bfloat16 [512, 2048], replicated, may hold values from -0.25 to 0.25
- conv_weight: bfloat16 [3, 3, 1024], replicated, may hold values from -2 to 2
- conv_bias: float32 [1024], replicated, may hold values from 0.5 to 2.5
- xproj_weight: bfloat16 [1024, 256], replicated, may hold values from -1 to 1
- dt_weight: bfloat16 [4, 32, 1024], replicated, may hold values from -2 to 1.5
- dt_bias: float32 [4, 1024], replicated, may hold values from -7 to -2
- a_log: float32 [4, 1024, 16], replicated, may hold values from -2 to 2.8
- dskip: float32 [1024], replicated, may hold values from 0.5 to 1.5
- out_gain: float32 [1024], replicated, may hold values from 0.1 to 1.9
- out_weight: bfloat16 [1024, 512], replicated, may hold values from -0.1875 to 0.1875
- seg_weight: bfloat16 [3, 3, 512, 16], replicated, may hold values from -0.09375 to 0.09375
- seg_bias: float32 [16], replicated, may hold values from -3 to 3
- edge_weight: bfloat16 [3, 3, 512, 2], replicated, may hold values from -0.09375 to 0.09375
- edge_bias: float32 [2], replicated, may hold values from -3 to 3
Outputs:
- block: bfloat16 [64, 512, 512], P('row', 'col')
- class_logits: float32 [64, 512, 16], P('row', 'col')
- edge_logits: float32 [64, 512, 2], P('row', 'col')
All inputs are finite; a program needn't handle non-finite values.
Results may differ from a plain program's by a relative error of at most 0.0065.
Values may be sent and summed in bfloat16 or wider, within the bound.
A program may use at most 128 MiB of HBM per device.

v0:
```python
import functools

import jax
import jax.numpy as jnp
from jax import lax
from jax.experimental import pallas as pl
from jax.experimental.pallas import tpu as pltpu
from jax.sharding import PartitionSpec as P

EPS = 1e-05
LOG2E = 1.4426950408889634
LANES = 128
SUB = 8


def extended(cells, sides, width):
    for axis, dim in sides:
        count = lax.axis_size(axis)
        ends = count - 1
        head = lax.slice_in_dim(cells, 0, width, axis=dim)
        tail = lax.slice_in_dim(cells, cells.shape[dim] - width, cells.shape[dim], axis=dim)
        cells = jnp.concatenate(
            [
                lax.ppermute(tail, axis, [(i, (i + 1) % count) for i in range(ends)]),
                cells,
                lax.ppermute(head, axis, [((i + 1) % count, i) for i in range(ends)]),
            ],
            axis=dim,
        )
    return cells


def layer_norm(values, gain):
    values = values.astype(jnp.float32)
    centred = values - jnp.mean(values, -1, keepdims=True)
    spread = jnp.mean(centred * centred, -1, keepdims=True)
    return centred * lax.rsqrt(spread + EPS) * gain


def step_sizes(lowrank, weight, bias):
    drive = jnp.dot(lowrank, weight, preferred_element_type=jnp.float32) + bias
    return jnp.maximum(drive, 0.0) + jnp.log1p(jnp.exp(-jnp.abs(drive)))


def line_kernel(states, pack_ref, wide_ref, bias_ref, rate_ref, out_ref, bc_ref, d_ref, u_ref, y_ref):
    tokens = pack_ref.shape[0]
    proj = pack_ref[:, LANES:]
    x = pack_ref[:, :LANES].astype(jnp.float32)
    for k in range(2):
        delta = step_sizes(proj, wide_ref[k], bias_ref[k : k + 1, :])
        d_ref[k] = delta
        u_ref[k] = delta * x
    bc_ref[...] = jnp.transpose(proj.astype(jnp.float32))
    rates = [rate_ref[k] for k in range(2)]
    half = LANES // 2

    def block(number, carry):
        places = [number * LANES, tokens - LANES - number * LANES]
        mats = []
        for k in range(2):
            first = pl.multiple_of(places[k], LANES)
            base = k * half + half - 2 * states
            both = bc_ref[base : base + 2 * states, pl.ds(first, LANES)]
            mats.append(both)

        def steps(turn, carry):
            held, mats = carry
            held = list(held)
            mats = list(mats)
            for j in range(SUB):
                for k in range(2):
                    if k == 0:
                        token = places[0] + turn * SUB + j
                        lane = j
                    else:
                        token = places[1] + LANES - 1 - (turn * SUB + j)
                        lane = LANES - 1 - j
                    d_row = d_ref[k, pl.ds(token, 1), :]
                    u_row = u_ref[k, pl.ds(token, 1), :]
                    b_col = mats[k][:states, lane : lane + 1]
                    c_col = mats[k][states:, lane : lane + 1]
                    held[k] = jnp.exp2(d_row * rates[k]) * held[k] + u_row * b_col
                    part = held[k] * c_col
                    total = part[:SUB]
                    for n in range(1, states // SUB):
                        total = total + part[n * SUB : (n + 1) * SUB]
                    y_ref[k, pl.ds(pl.multiple_of(token * SUB, SUB), SUB), :] = total
            mats[0] = pltpu.roll(mats[0], LANES - SUB, 1)
            mats[1] = pltpu.roll(mats[1], SUB, 1)
            return (tuple(held), tuple(mats))

        held, _ = lax.fori_loop(0, LANES // SUB, steps, (carry, tuple(mats)))
        return held

    start = jnp.zeros((states, LANES), jnp.float32)
    lax.fori_loop(0, tokens // LANES, block, (start, start))

    for first in range(0, tokens, LANES):
        total = None
        for k in range(2):
            for s in range(SUB):
                piece = y_ref[k, pl.ds(first * SUB + s, LANES, stride=SUB), :]
                total = piece if total is None else total + piece
        out_ref[first : first + LANES, :] = total.astype(out_ref.dtype)


def column_kernel(states, pack_ref, bc_ref, wide_ref, bias_ref, rate_ref, out_ref, d_ref, u_ref, y_ref):
    tokens = pack_ref.shape[0]
    inner = out_ref.shape[1]
    groups = inner // LANES
    proj = pack_ref[:, inner:]
    for g in range(groups):
        lanes = slice(g * LANES, (g + 1) * LANES)
        x = pack_ref[:, lanes].astype(jnp.float32)
        for k in range(2):
            delta = step_sizes(proj, wide_ref[k, :, lanes], bias_ref[k : k + 1, lanes])
            d_ref[k, pl.ds(g, tokens, stride=groups), :] = delta
            u_ref[k, pl.ds(g, tokens, stride=groups), :] = delta * x
    for k in range(2):

        def step(turn, held, k=k):
            token = turn if k == 0 else tokens - 1 - turn
            rows = pl.ds(pl.multiple_of(token * groups, groups), groups)
            d_now = d_ref[k, rows, :]
            u_now = u_ref[k, rows, :]
            total = None
            after = []
            for n in range(states):
                state = jnp.exp2(d_now * rate_ref[k, n]) * held[n]
                state = state + u_now * bc_ref[token, 2 * k * states + n]
                part = state * bc_ref[token, (2 * k + 1) * states + n]
                total = part if total is None else total + part
                after.append(state)
            if k == 0:
                y_ref[rows, :] = total
            else:
                y_ref[rows, :] = y_ref[rows, :] + total
            return tuple(after)

        start = jnp.zeros((groups, LANES), jnp.float32)
        lax.fori_loop(0, tokens, step, (start,) * states, unroll=2)
    for g in range(groups):
        out_ref[:, g * LANES : (g + 1) * LANES] = y_ref[
            pl.ds(g, tokens, stride=groups), :
        ].astype(out_ref.dtype)


def on_device(
    feat,
    ln_gain,
    in_weight,
    conv_weight,
    conv_bias,
    xproj_weight,
    dt_weight,
    dt_bias,
    a_log,
    dskip,
    out_gain,
    out_weight,
    seg_weight,
    seg_bias,
    edge_weight,
    edge_bias,
):
    rows, cols, width = feat.shape
    inner = conv_weight.shape[-1]
    states = a_log.shape[-1]
    rank = dt_weight.shape[1]
    packed = xproj_weight.shape[1] // 4
    slices = inner // LANES
    down = lax.axis_size("row")
    along = lax.axis_size("col")
    vmem = pl.BlockSpec(memory_space=pltpu.VMEM)

    rates = jnp.transpose(-jnp.exp(a_log) * LOG2E, (0, 2, 1))
    place = (lax.axis_index("col") // rows) * LANES
    empty = jnp.zeros((rank, inner), dt_weight.dtype)
    wide = []
    for pair in range(2):
        for k in range(2):
            at = k * packed
            wide.append(
                jnp.pad(dt_weight[2 * pair + k], ((at, 2 * packed - at - rank), (0, 0)))
            )
    wide = jnp.stack(wide)
    wide_line = lax.dynamic_slice_in_dim(wide[:2], place, LANES, 2)
    bias_line = lax.dynamic_slice_in_dim(dt_bias[:2], place, LANES, 1)
    rate_line = lax.dynamic_slice_in_dim(rates[:2], place, LANES, 2)
    rate_column = rates[2:].reshape(2, states, slices, LANES)

    framed = extended(feat, (("row", 0), ("col", 1)), 1)
    normed = layer_norm(framed, ln_gain).astype(jnp.bfloat16)
    xin = jnp.dot(
        normed.reshape(-1, width), in_weight[:, :inner], preferred_element_type=jnp.float32
    )
    xin = xin.astype(jnp.bfloat16).reshape(rows + 2, cols + 2, inner).astype(jnp.float32)
    gate = jnp.dot(
        normed[1:-1, 1:-1].reshape(-1, width),
        in_weight[:, inner:],
        preferred_element_type=jnp.float32,
    ).astype(jnp.bfloat16)
    mixed = jnp.zeros((rows, cols, inner), jnp.float32)
    for i in range(3):
        for j in range(3):
            mixed = mixed + xin[i : i + rows, j : j + cols] * conv_weight[i, j].astype(jnp.float32)
    xconv = jax.nn.silu(mixed + conv_bias).astype(jnp.bfloat16)
    proj = jnp.dot(
        xconv.reshape(rows * cols, inner), xproj_weight, preferred_element_type=jnp.float32
    ).astype(jnp.bfloat16).reshape(rows, cols, 4 * packed)

    line_x = jnp.transpose(xconv.reshape(rows, cols, slices, LANES), (2, 0, 1, 3))
    line_p = jnp.broadcast_to(proj[None, :, :, : 2 * packed], (slices, rows, cols, 2 * packed))
    line_in = jnp.concatenate([line_x, line_p], -1).reshape(along, cols, 2 * LANES)
    line_in = lax.all_to_all(line_in, "col", 0, 0, tiled=True).reshape(along * cols, 2 * LANES)
    column_in = jnp.concatenate([xconv, proj[:, :, 2 * packed :]], -1)
    column_in = jnp.swapaxes(column_in, 0, 1)
    column_in = lax.all_to_all(column_in, "row", 0, 0, tiled=True).reshape(down * rows, -1)

    line_tokens = along * cols
    line_out = pl.pallas_call(
        functools.partial(line_kernel, states),
        out_shape=jax.ShapeDtypeStruct((line_tokens, LANES), jnp.bfloat16),
        in_specs=[vmem] * 4,
        out_specs=vmem,
        scratch_shapes=[
            pltpu.VMEM((LANES, line_tokens), jnp.float32),
            pltpu.VMEM((2, line_tokens, LANES), jnp.float32),
            pltpu.VMEM((2, line_tokens, LANES), jnp.float32),
            pltpu.VMEM((2, line_tokens * SUB, LANES), jnp.float32),
        ],
        name="lines",
    )(line_in, wide_line, bias_line, rate_line)

    column_tokens = down * rows
    own = column_in[:, inner:].astype(jnp.float32).reshape(column_tokens, 2, packed)
    scalars = own[:, :, rank:].reshape(column_tokens, 4 * states)
    column_out = pl.pallas_call(
        functools.partial(column_kernel, states),
        out_shape=jax.ShapeDtypeStruct((column_tokens, inner), jnp.bfloat16),
        in_specs=[vmem, pl.BlockSpec(memory_space=pltpu.SMEM), vmem, vmem, vmem],
        out_specs=vmem,
        scratch_shapes=[
            pltpu.VMEM((2, column_tokens * slices, LANES), jnp.float32),
            pltpu.VMEM((2, column_tokens * slices, LANES), jnp.float32),
            pltpu.VMEM((column_tokens * slices, LANES), jnp.float32),
        ],
        name="columns",
    )(column_in, scalars, wide[2:], dt_bias[2:], rate_column)

    line_out = lax.all_to_all(line_out.reshape(along, cols, LANES), "col", 0, 0, tiled=True)
    line_out = jnp.transpose(line_out.reshape(slices, rows, cols, LANES), (1, 2, 0, 3)).reshape(
        rows, cols, inner
    )
    column_out = lax.all_to_all(column_out.reshape(down, rows, inner), "row", 0, 0, tiled=True)
    column_out = jnp.swapaxes(column_out, 0, 1)

    total = line_out.astype(jnp.float32) + column_out.astype(jnp.float32)
    total = total + dskip * xconv.astype(jnp.float32)
    gate = gate.reshape(rows, cols, inner)
    gated = (layer_norm(total, out_gain) * jax.nn.silu(gate.astype(jnp.float32))).astype(
        jnp.bfloat16
    )
    projected = jnp.dot(
        gated.reshape(rows * cols, inner), out_weight, preferred_element_type=jnp.float32
    ).reshape(rows, cols, width)
    block = (feat.astype(jnp.float32) + projected).astype(jnp.bfloat16)
    border = extended(block, (("row", 0), ("col", 1)), 1)
    patches = jnp.concatenate(
        [border[i : i + rows, j : j + cols] for i in range(3) for j in range(3)], axis=-1
    ).reshape(rows * cols, 9 * width)
    classes = seg_weight.shape[-1]
    filters = jnp.concatenate([seg_weight, edge_weight], axis=-1).reshape(9 * width, -1)
    logits = jnp.dot(patches, filters, preferred_element_type=jnp.float32)
    class_logits = logits[:, :classes].reshape(rows, cols, classes) + seg_bias
    edge_logits = logits[:, classes:].reshape(rows, cols, -1) + edge_bias
    return (block, class_logits, edge_logits)


def solution(mesh):
    tile = P("row", "col", None)
    return jax.shard_map(
        on_device,
        mesh=mesh,
        in_specs=(tile,) + (P(),) * 15,
        out_specs=(tile, tile, tile),
        check_vma=False,
    )
```

profile of v0, /device:TPU:72, one launch (start us, length us, event | category | flops | bytes accessed | tf_op | source)
XLA Modules:
  0.0 125.2 jit_solution(4220231164829983778)
XLA Ops:
  0.7 0.8 fusion.40
  1.5 1.9 %collective-permute-start = (bf16[1,16,512]{2,1,0:T(8,128)(2,1)S(1)}, bf16[1,16,512]{2,1,0:T(8,128)(2,1)S(1)}, u32[]{:S(2)}, u32[]{:S(2)}) collective-permute-start(bf16[1,16,512]{2,1,0:T(8,128)(2,1)S(1)} %get-tuple-element.34), channel_id=1, source_target_pairs={{0,32},{32,64},{64,96},{96,128},{128,160},{160,192},{192,224},{224... | collective-permute-start | bytes 49160 | tf_op jit(solution)/shard_map/ppermute | solution.py:24
  3.4 3.6 %collective-permute-start.1 = (bf16[1,16,512]{2,1,0:T(8,128)(2,1)S(1)}, bf16[1,16,512]{2,1,0:T(8,128)(2,1)S(1)}, u32[]{:S(2)}, u32[]{:S(2)}) collective-permute-start(bf16[1,16,512]{2,1,0:T(8,128)(2,1)S(1)} %get-tuple-element.33), channel_id=1, source_target_pairs={{32,0},{64,32},{96,64},{128,96},{160,128},{192,160},{224,192},{256... | collective-permute-start | bytes 49160 | tf_op jit(solution)/shard_map/ppermute | solution.py:26
  7.1 0.9 slice_convert_fusion.8
  8.0 1.0 slice_bitcast_fusion.1
  8.9 1.0 multiply_bitcast_fusion
  10.1 3.8 %collective-permute-start.3 = (bf16[6,1,512]{2,1,0:T(2,128)(2,1)S(1)}, bf16[6,1,512]{2,1,0:T(2,128)(2,1)S(1)}, u32[]{:S(2)}, u32[]{:S(2)}) collective-permute-start(bf16[6,1,512]{2,1,0:T(2,128)(2,1)S(1)} %get-tuple-element.30), channel_id=1, source_target_pairs={{1,0},{2,1},{3,2},{4,3},{5,4},{6,5},{7,6},{8,7},{9,8},{10,9},{11,1... | collective-permute-start | bytes 18440 | tf_op jit(solution)/shard_map/ppermute | solution.py:26
  13.9 2.1 %collective-permute-start.2 = (bf16[6,1,512]{2,1,0:T(2,128)(2,1)S(1)}, bf16[6,1,512]{2,1,0:T(2,128)(2,1)S(1)}, u32[]{:S(2)}, u32[]{:S(2)}) collective-permute-start(bf16[6,1,512]{2,1,0:T(2,128)(2,1)S(1)} %get-tuple-element.29), channel_id=1, source_target_pairs={{0,1},{1,2},{2,3},{3,4},{4,5},{5,6},{6,7},{7,8},{8,9},{9,10},{10,1... | collective-permute-start | bytes 18440 | tf_op jit(solution)/shard_map/ppermute | solution.py:24
  16.0 0.7 fusion.30.wide_ref
  16.7 4.9 %collective-permute-done.2 = bf16[6,1,512]{2,1,0:T(2,128)(2,1)S(1)} collective-permute-done((bf16[6,1,512]{2,1,0:T(2,128)(2,1)S(1)}, bf16[6,1,512]{2,1,0:T(2,128)(2,1)S(1)}, u32[]{:S(2)}, u32[]{:S(2)}) %collective-permute-start.2) | collective-permute-done | bytes 6176 | tf_op jit(solution)/shard_map/ppermute | solution.py:24
  21.6 0.1 fusion.34
  21.8 0.2 multiply_reduce_fusion
  22.2 1.6 %fusion = f32[108,1024]{1,0:T(8,128)S(1)} fusion(bf16[512,2048]{1,0:T(8,128)(2,1)} %param.18, f32[108,512]{1,0:T(8,128)S(1)} %reshape.138, f32[512]{0:T(512)S(1)} %copy-done.10, f32[108]{0:T(128)S(1)} %rsqrt.21, f32[108]{0:T(128)S(1)} %div.30), kind=kOutput, calls=%fused_computation.1 | convolution fusion | flops 113688576 | bytes 1715040 | tf_op jit(solution)/shard_map/dot_general | solution.py:194
  23.9 0.3 multiply_convert_fusion
  24.2 0.7 copy-done.4
  24.8 0.2 convolution_convert_fusion.2
  25.2 0.7 copy.55
  25.9 11.3 %all-to-all-start = ((bf16[32,16,256]{2,1,0:T(8,128)(2,1)}), bf16[32,16,256]{2,1,0:T(8,128)(2,1)S(1)}, u32[]{:S(2)}, u32[]{:S(2)}) async-start(bf16[32,16,256]{2,1,0:T(8,128)(2,1)} %bitcast.12), calls=%async_computation | async-start | bytes 524288 | tf_op jit(solution)/shard_map/all_to_all | solution.py:215
  37.2 0.6 constant_dynamic-slice_fusion.rate_ref
  37.9 0.6 fusion.42
  38.5 0.7 copy.57
  39.2 8.9 %all-to-all-done = bf16[32,16,256]{2,1,0:T(8,128)(2,1)S(1)} async-done(((bf16[32,16,256]{2,1,0:T(8,128)(2,1)}), bf16[32,16,256]{2,1,0:T(8,128)(2,1)S(1)}, u32[]{:S(2)}, u32[]{:S(2)}) %all-to-all-start) | async-done | bytes 262176 | tf_op jit(solution)/shard_map/all_to_all | solution.py:215
  48.1 8.7 %all-to-all-start.2 = ((bf16[16,4,1152]{2,1,0:T(4,128)(2,1)}), bf16[16,4,1152]{2,1,0:T(4,128)(2,1)S(1)}, u32[]{:S(2)}, u32[]{:S(2)}) async-start(bf16[16,4,1152]{2,1,0:T(4,128)(2,1)} %copy.57), calls=%async_computation.2 | async-start | bytes 294912 | tf_op jit(solution)/shard_map/all_to_all | solution.py:218
  56.8 0.6 constant_dynamic-slice_fusion.1.bias_ref
  57.4 0.7 copy.67
  58.1 0.8 pad_maximum_fusion.wide_ref
  59.0 13.6 %lines.1 = bf16[512,128]{1,0:T(8,128)(2,1)} custom-call(bf16[512,256]{1,0:T(8,128)(2,1)} %bitcast.81, bf16[2,128,128]{2,1,0:T(8,128)(2,1)} %fusion.30.wide_ref, f32[2,128]{1,0:T(2,128)} %constant_dynamic-slice_fusion.1.bias_ref, f32[2,16,128]{2,1,0:T(8,128)} %constant_dynamic-slice_fusion.rate_ref), custom_call_target="tpu_custom_call" | custom-call | tf_op jit(solution)/shard_map/lines/pallas_call | solution.py:221
  72.6 4.6 %all-to-all-start.1 = ((bf16[32,16,128]{2,1,0:T(8,128)(2,1)}), bf16[32,16,128]{2,1,0:T(8,128)(2,1)S(1)}, u32[]{:S(2)}, u32[]{:S(2)}) async-start(bf16[32,16,128]{2,1,0:T(8,128)(2,1)} %bitcast.87), calls=%async_computation.1 | async-start | bytes 262144 | tf_op jit(solution)/shard_map/all_to_all | solution.py:251
  77.5 0.7 copy.59.bc_ref
  78.2 5.7 %columns.1 = bf16[64,1024]{1,0:T(8,128)(2,1)} custom-call(bf16[64,1152]{1,0:T(8,128)(2,1)} %copy-done.3, f32[64,64]{1,0:T(8,128)} %copy.59.bc_ref, bf16[2,128,1024]{2,1,0:T(8,128)(2,1)} %pad_maximum_fusion.wide_ref, f32[2,1024]{1,0:T(2,128)} %get-tuple-element.46.bias_ref, f32[2,16,8,128]{3,2,1,0:T(8,128)} %bitcast.88), custom_call_target="tpu_custom_call" | custom-call | tf_op jit(solution)/shard_map/columns/pallas_call | solution.py:238
  83.9 1.6 %reshape.132 = bf16[16,4,1024]{2,1,0:T(4,128)(2,1)} reshape(bf16[64,1024]{1,0:T(8,128)(2,1)} %columns.1) | data formatting | bytes 262144 | tf_op jit(solution)/shard_map/reshape | solution.py:255
  85.5 1.6 %all-to-all-done.1 = bf16[32,16,128]{2,1,0:T(8,128)(2,1)S(1)} async-done(((bf16[32,16,128]{2,1,0:T(8,128)(2,1)}), bf16[32,16,128]{2,1,0:T(8,128)(2,1)S(1)}, u32[]{:S(2)}, u32[]{:S(2)}) %all-to-all-start.1) | async-done | bytes 131104 | tf_op jit(solution)/shard_map/all_to_all | solution.py:251
  87.1 7.2 %all-to-all-start.3 = ((bf16[16,4,1024]{2,1,0:T(4,128)(2,1)}), bf16[16,4,1024]{2,1,0:T(4,128)(2,1)S(1)}, u32[]{:S(2)}, u32[]{:S(2)}) async-start(bf16[16,4,1024]{2,1,0:T(4,128)(2,1)} %reshape.132), calls=%async_computation.3 | async-start | bytes 262144 | tf_op jit(solution)/shard_map/all_to_all | solution.py:255
  94.3 1.5 %convolution_convert_fusion.1 = bf16[64,1024]{1,0:T(8,128)(2,1)S(1)} fusion(bf16[64,512]{1,0:T(8,128)(2,1)S(1)} %bitcast.92, bf16[512,2048]{1,0:T(8,128)(2,1)} %param.18), kind=kOutput, calls=%fused_computation.2 | convolution fusion | flops 67174400 | bytes 1245184 | tf_op jit(solution)/shard_map/dot_general | solution.py:198
  96.0 5.7 %all-to-all-done.3 = bf16[16,4,1024]{2,1,0:T(4,128)(2,1)S(1)} async-done(((bf16[16,4,1024]{2,1,0:T(4,128)(2,1)}), bf16[16,4,1024]{2,1,0:T(4,128)(2,1)S(1)}, u32[]{:S(2)}, u32[]{:S(2)}) %all-to-all-start.3) | async-done | bytes 131104 | tf_op jit(solution)/shard_map/all_to_all | solution.py:255
  101.7 0.5 fusion.35
  102.2 0.2 multiply_reduce_fusion.1
  102.4 0.4 fusion.1
  102.8 3.7 %collective-permute-start.5 = (bf16[1,16,512]{2,1,0:T(8,128)(2,1)S(1)}, bf16[1,16,512]{2,1,0:T(8,128)(2,1)S(1)}, u32[]{:S(2)}, u32[]{:S(2)}) collective-permute-start(bf16[1,16,512]{2,1,0:T(8,128)(2,1)S(1)} %get-tuple-element.32), channel_id=1, source_target_pairs={{32,0},{64,32},{96,64},{128,96},{160,128},{192,160},{224,192},{256... | collective-permute-start | bytes 49160 | tf_op jit(solution)/shard_map/ppermute | solution.py:26
  106.5 1.9 %collective-permute-start.4 = (bf16[1,16,512]{2,1,0:T(8,128)(2,1)S(1)}, bf16[1,16,512]{2,1,0:T(8,128)(2,1)S(1)}, u32[]{:S(2)}, u32[]{:S(2)}) collective-permute-start(bf16[1,16,512]{2,1,0:T(8,128)(2,1)S(1)} %get-tuple-element.31), channel_id=1, source_target_pairs={{0,32},{32,64},{64,96},{96,128},{128,160},{160,192},{192,224},{224... | collective-permute-start | bytes 49160 | tf_op jit(solution)/shard_map/ppermute | solution.py:24
  108.5 3.1 %collective-permute-done.4 = bf16[1,16,512]{2,1,0:T(8,128)(2,1)S(1)} collective-permute-done((bf16[1,16,512]{2,1,0:T(8,128)(2,1)S(1)}, bf16[1,16,512]{2,1,0:T(8,128)(2,1)S(1)}, u32[]{:S(2)}, u32[]{:S(2)}) %collective-permute-start.4) | collective-permute-done | bytes 16416 | tf_op jit(solution)/shard_map/ppermute | solution.py:24
  111.6 3.9 %collective-permute-start.7 = (bf16[6,1,512]{2,1,0:T(2,128)(2,1)S(1)}, bf16[6,1,512]{2,1,0:T(2,128)(2,1)S(1)}, u32[]{:S(2)}, u32[]{:S(2)}) collective-permute-start(bf16[6,1,512]{2,1,0:T(2,128)(2,1)S(1)} %get-tuple-element.27), channel_id=1, source_target_pairs={{1,0},{2,1},{3,2},{4,3},{5,4},{6,5},{7,6},{8,7},{9,8},{10,9},{11,1... | collective-permute-start | bytes 18440 | tf_op jit(solution)/shard_map/ppermute | solution.py:26
  115.5 2.0 %collective-permute-start.6 = (bf16[6,1,512]{2,1,0:T(2,128)(2,1)S(1)}, bf16[6,1,512]{2,1,0:T(2,128)(2,1)S(1)}, u32[]{:S(2)}, u32[]{:S(2)}) collective-permute-start(bf16[6,1,512]{2,1,0:T(2,128)(2,1)S(1)} %get-tuple-element.28), channel_id=1, source_target_pairs={{0,1},{1,2},{2,3},{3,4},{4,5},{5,6},{6,7},{7,8},{8,9},{9,10},{10,1... | collective-permute-start | bytes 18440 | tf_op jit(solution)/shard_map/ppermute | solution.py:24
  117.6 0.2 reshape.135
  117.9 5.3 %collective-permute-done.6 = bf16[6,1,512]{2,1,0:T(2,128)(2,1)S(1)} collective-permute-done((bf16[6,1,512]{2,1,0:T(2,128)(2,1)S(1)}, bf16[6,1,512]{2,1,0:T(2,128)(2,1)S(1)}, u32[]{:S(2)}, u32[]{:S(2)}) %collective-permute-start.6) | collective-permute-done | bytes 6176 | tf_op jit(solution)/shard_map/ppermute | solution.py:24
  123.4 0.3 fusion.43
  123.9 0.6 copy.63
  124.6 0.6 broadcast_add_fusion
  (85 shorter events, 1.7 us)
Async XLA Ops:
  0.6 101.8 %copy-start = (bf16[1024,512]{1,0:T(8,128)(2,1)S(1)}, bf16[1024,512]{1,0:T(8,128)(2,1)}, u32[]{:S(2)}) copy-start(bf16[1024,512]{1,0:T(8,128)(2,1)} %param.27) | copy-start | bytes 3145732
  0.6 9.4 %copy-start.6 = (bf16[4,16,512]{2,1,0:T(8,128)(2,1)S(1)}, bf16[4,16,512]{2,1,0:T(8,128)(2,1)}, u32[]{:S(2)}) copy-start(bf16[4,16,512]{2,1,0:T(8,128)(2,1)} %param.16) | copy-start | bytes 196612
  1.5 8.5 %collective-permute-start = (bf16[1,16,512]{2,1,0:T(8,128)(2,1)S(1)}, bf16[1,16,512]{2,1,0:T(8,128)(2,1)S(1)}, u32[]{:S(2)}, u32[]{:S(2)}) collective-permute-start(bf16[1,16,512]{2,1,0:T(8,128)(2,1)S(1)} %get-tuple-element.34), channel_id=1, source_target_pairs={{0,32},{32,64},{64,96},{96,128},{128,160},{160,192},{192,224},{224... | collective-permute-start | bytes 49160 | tf_op jit(solution)/shard_map/ppermute | solution.py:24
  3.4 6.7 %collective-permute-start.1 = (bf16[1,16,512]{2,1,0:T(8,128)(2,1)S(1)}, bf16[1,16,512]{2,1,0:T(8,128)(2,1)S(1)}, u32[]{:S(2)}, u32[]{:S(2)}) collective-permute-start(bf16[1,16,512]{2,1,0:T(8,128)(2,1)S(1)} %get-tuple-element.33), channel_id=1, source_target_pairs={{32,0},{64,32},{96,64},{128,96},{160,128},{192,160},{224,192},{256... | collective-permute-start | bytes 49160 | tf_op jit(solution)/shard_map/ppermute | solution.py:26
  8.9 13.3 %copy-start.10 = (f32[512]{0:T(512)S(1)}, f32[512]{0:T(512)}, u32[]{:S(2)}) copy-start(f32[512]{0:T(512)} %param.17) | copy-start | bytes 6148
  10.1 6.5 %collective-permute-start.3 = (bf16[6,1,512]{2,1,0:T(2,128)(2,1)S(1)}, bf16[6,1,512]{2,1,0:T(2,128)(2,1)S(1)}, u32[]{:S(2)}, u32[]{:S(2)}) collective-permute-start(bf16[6,1,512]{2,1,0:T(2,128)(2,1)S(1)} %get-tuple-element.30), channel_id=1, source_target_pairs={{1,0},{2,1},{3,2},{4,3},{5,4},{6,5},{7,6},{8,7},{9,8},{10,9},{11,1... | collective-permute-start | bytes 18440 | tf_op jit(solution)/shard_map/ppermute | solution.py:26
  13.9 7.7 %collective-permute-start.2 = (bf16[6,1,512]{2,1,0:T(2,128)(2,1)S(1)}, bf16[6,1,512]{2,1,0:T(2,128)(2,1)S(1)}, u32[]{:S(2)}, u32[]{:S(2)}) collective-permute-start(bf16[6,1,512]{2,1,0:T(2,128)(2,1)S(1)} %get-tuple-element.29), channel_id=1, source_target_pairs={{0,1},{1,2},{2,3},{3,4},{4,5},{5,6},{6,7},{7,8},{8,9},{9,10},{10,1... | collective-permute-start | bytes 18440 | tf_op jit(solution)/shard_map/ppermute | solution.py:24
  21.8 2.0 %copy-start.8 = (f32[1024]{0:T(1024)S(1)}, f32[1024]{0:T(1024)}, u32[]{:S(2)}) copy-start(f32[1024]{0:T(1024)} %param.20) | copy-start | bytes 12292
  23.8 1.0 copy-start.4
  24.2 13.7 %copy-start.9 = (f32[4,1024]{1,0:T(4,128)S(1)}, f32[4,1024]{1,0:T(4,128)}, u32[]{:S(2)}) copy-start(f32[4,1024]{1,0:T(4,128)} %param.23) | copy-start | bytes 49156
  25.9 22.2 %all-to-all-start = ((bf16[32,16,256]{2,1,0:T(8,128)(2,1)}), bf16[32,16,256]{2,1,0:T(8,128)(2,1)S(1)}, u32[]{:S(2)}, u32[]{:S(2)}) async-start(bf16[32,16,256]{2,1,0:T(8,128)(2,1)} %bitcast.12), calls=%async_computation | async-start | bytes 524288 | tf_op jit(solution)/shard_map/all_to_all | solution.py:215
  48.1 10.9 %copy-start.2 = (bf16[32,16,256]{2,1,0:T(8,128)(2,1)}, bf16[32,16,256]{2,1,0:T(8,128)(2,1)S(1)}, u32[]{:S(2)}) copy-start(bf16[32,16,256]{2,1,0:T(8,128)(2,1)S(1)} %all-to-all-done) | copy-start | bytes 786436
  48.1 24.4 %all-to-all-start.2 = ((bf16[16,4,1152]{2,1,0:T(4,128)(2,1)}), bf16[16,4,1152]{2,1,0:T(4,128)(2,1)S(1)}, u32[]{:S(2)}, u32[]{:S(2)}) async-start(bf16[16,4,1152]{2,1,0:T(4,128)(2,1)} %copy.57), calls=%async_computation.2 | async-start | bytes 294912 | tf_op jit(solution)/shard_map/all_to_all | solution.py:218
  72.6 14.5 %all-to-all-start.1 = ((bf16[32,16,128]{2,1,0:T(8,128)(2,1)}), bf16[32,16,128]{2,1,0:T(8,128)(2,1)S(1)}, u32[]{:S(2)}, u32[]{:S(2)}) async-start(bf16[32,16,128]{2,1,0:T(8,128)(2,1)} %bitcast.87), calls=%async_computation.1 | async-start | bytes 262144 | tf_op jit(solution)/shard_map/all_to_all | solution.py:251
  77.3 24.5 %copy-start.11 = (f32[1024]{0:T(1024)S(1)}, f32[1024]{0:T(1024)}, u32[]{:S(2)}) copy-start(f32[1024]{0:T(1024)} %param.25) | copy-start | bytes 12292
  77.3 0.9 copy-start.3
  87.1 14.6 %all-to-all-start.3 = ((bf16[16,4,1024]{2,1,0:T(4,128)(2,1)}), bf16[16,4,1024]{2,1,0:T(4,128)(2,1)S(1)}, u32[]{:S(2)}, u32[]{:S(2)}) async-start(bf16[16,4,1024]{2,1,0:T(4,128)(2,1)} %reshape.132), calls=%async_computation.3 | async-start | bytes 262144 | tf_op jit(solution)/shard_map/all_to_all | solution.py:255
  95.9 6.6 %copy-start.14 = (f32[1024]{0:T(1024)S(1)}, f32[1024]{0:T(1024)}, u32[]{:S(2)}) copy-start(f32[1024]{0:T(1024)} %param.26) | copy-start | bytes 12292
  102.2 15.3 %copy-start.5 = (bf16[3,3,512,16]{2,3,1,0:T(8,128)(2,1)S(1)}, bf16[3,3,512,16]{2,3,1,0:T(8,128)(2,1)}, u32[]{:S(2)}) copy-start(bf16[3,3,512,16]{2,3,1,0:T(8,128)(2,1)} %param.28) | copy-start | bytes 442372
  102.2 15.3 %copy-start.7 = (bf16[3,3,512,2]{2,3,1,0:T(2,128)(2,1)S(1)}, bf16[3,3,512,2]{2,3,1,0:T(2,128)(2,1)}, u32[]{:S(2)}) copy-start(bf16[3,3,512,2]{2,3,1,0:T(2,128)(2,1)} %param.30) | copy-start | bytes 55300
  102.8 22.4 %copy-start.1 = (bf16[4,16,512]{2,1,0:T(8,128)(2,1)}, bf16[4,16,512]{2,1,0:T(8,128)(2,1)S(1)}, u32[]{:S(2)}) copy-start(bf16[4,16,512]{2,1,0:T(8,128)(2,1)S(1)} %fusion.1) | copy-start | bytes 196612
  102.8 21.1 %copy-start.13 = (f32[2]{0:T(128)S(1)}, f32[2]{0:T(128)}, u32[]{:S(2)}) copy-start(f32[2]{0:T(128)} %param.31) | copy-start | bytes 28
  102.8 21.7 %copy-start.12 = (f32[16]{0:T(128)S(1)}, f32[16]{0:T(128)}, u32[]{:S(2)}) copy-start(f32[16]{0:T(128)} %param.29) | copy-start | bytes 196
  102.8 5.6 %collective-permute-start.5 = (bf16[1,16,512]{2,1,0:T(8,128)(2,1)S(1)}, bf16[1,16,512]{2,1,0:T(8,128)(2,1)S(1)}, u32[]{:S(2)}, u32[]{:S(2)}) collective-permute-start(bf16[1,16,512]{2,1,0:T(8,128)(2,1)S(1)} %get-tuple-element.32), channel_id=1, source_target_pairs={{32,0},{64,32},{96,64},{128,96},{160,128},{192,160},{224,192},{256... | collective-permute-start | bytes 49160 | tf_op jit(solution)/shard_map/ppermute | solution.py:26
  106.5 5.1 %collective-permute-start.4 = (bf16[1,16,512]{2,1,0:T(8,128)(2,1)S(1)}, bf16[1,16,512]{2,1,0:T(8,128)(2,1)S(1)}, u32[]{:S(2)}, u32[]{:S(2)}) collective-permute-start(bf16[1,16,512]{2,1,0:T(8,128)(2,1)S(1)} %get-tuple-element.31), channel_id=1, source_target_pairs={{0,32},{32,64},{64,96},{96,128},{128,160},{160,192},{192,224},{224... | collective-permute-start | bytes 49160 | tf_op jit(solution)/shard_map/ppermute | solution.py:24
  111.6 6.3 %collective-permute-start.7 = (bf16[6,1,512]{2,1,0:T(2,128)(2,1)S(1)}, bf16[6,1,512]{2,1,0:T(2,128)(2,1)S(1)}, u32[]{:S(2)}, u32[]{:S(2)}) collective-permute-start(bf16[6,1,512]{2,1,0:T(2,128)(2,1)S(1)} %get-tuple-element.27), channel_id=1, source_target_pairs={{1,0},{2,1},{3,2},{4,3},{5,4},{6,5},{7,6},{8,7},{9,8},{10,9},{11,1... | collective-permute-start | bytes 18440 | tf_op jit(solution)/shard_map/ppermute | solution.py:26
  115.5 7.7 %collective-permute-start.6 = (bf16[6,1,512]{2,1,0:T(2,128)(2,1)S(1)}, bf16[6,1,512]{2,1,0:T(2,128)(2,1)S(1)}, u32[]{:S(2)}, u32[]{:S(2)}) collective-permute-start(bf16[6,1,512]{2,1,0:T(2,128)(2,1)S(1)} %get-tuple-element.28), channel_id=1, source_target_pairs={{0,1},{1,2},{2,3},{3,4},{4,5},{5,6},{6,7},{7,8},{8,9},{9,10},{10,1... | collective-permute-start | bytes 18440 | tf_op jit(solution)/shard_map/ppermute | solution.py:24
where the time goes:
time: 126 us; the launch traced here: 125 us
  starting transfers between devices  54.6 us (43%)
  waiting for transfers between devices  29.6 us (23%)
  Pallas kernels  19.3 us (15%)
  local copies, waits for them, and re-layouts  10.9 us (9%)
  other arithmetic  5.67 us (4%)
  matrix products  3.91 us (3%)
  between operations  1.27 us (1%)
    ppermute x4, starting transfers between devices, extended(): lax.ppermute(head, axis, [((i + 1) % count, i) for i in range(ends)])  14.9 us
    pallas_call x1, Pallas kernels, on_device(): pl.pallas_call(functools.partial(line_kernel, states), out_shape=jax.Shap...  13.6 us
    ppermute x4, waiting for transfers between devices, extended(): lax.ppermute(tail, axis, [(i, (i + 1) % count) for i in range(ends)])  13.4 us
    all_to_all x1, starting transfers between devices, on_device(): lax.all_to_all(line_in, 'col', 0, 0, tiled=True)  11.3 us
    all_to_all x1, waiting for transfers between devices, on_device(): lax.all_to_all(line_in, 'col', 0, 0, tiled=True)  8.93 us
    all_to_all x1, starting transfers between devices, on_device(): lax.all_to_all(column_in, 'row', 0, 0, tiled=True).reshape(down * rows, -1)  8.68 us
    ppermute x4, starting transfers between devices, extended(): lax.ppermute(tail, axis, [(i, (i + 1) % count) for i in range(ends)])  7.88 us
    all_to_all x1, starting transfers between devices, on_device(): lax.all_to_all(column_out.reshape(down, rows, inner), 'row', 0, 0, tiled=...  7.22 us
  transfers between devices with their start and end apart: 12, of which 6 were waited for; matrix products, arithmetic and copies ran while one was open for 10% of the time, Pallas kernels for 15%

commit v1 on v0

--- a/solution.py
+++ b/solution.py
@@ -11,23 +11,155 @@
 LOG2E = 1.4426950408889634
 LANES = 128
 SUB = 8
-
-
-def extended(cells, sides, width):
-    for axis, dim in sides:
-        count = lax.axis_size(axis)
-        ends = count - 1
-        head = lax.slice_in_dim(cells, 0, width, axis=dim)
-        tail = lax.slice_in_dim(cells, cells.shape[dim] - width, cells.shape[dim], axis=dim)
-        cells = jnp.concatenate(
-            [
-                lax.ppermute(tail, axis, [(i, (i + 1) % count) for i in range(ends)]),
-                cells,
-                lax.ppermute(head, axis, [((i + 1) % count, i) for i in range(ends)]),
-            ],
-            axis=dim,
+MESH = pl.DeviceIdType.MESH
+
+
+def entry_barrier(axes):
+    barrier = pltpu.get_barrier_semaphore()
+    count = 0
+    for axis in axes:
+        size = lax.axis_size(axis)
+
+        def greet(i, carry, axis=axis, size=size):
+            other = lax.rem(lax.axis_index(axis) + i, size)
+            pl.semaphore_signal(barrier, inc=1, device_id={axis: other}, device_id_type=MESH)
+            return carry
+
+        lax.fori_loop(1, size, greet, 0)
+        count += size - 1
+    pl.semaphore_wait(barrier, count)
+
+
+def swap_kernel(line_ref, column_ref, line_got, column_got, own_sem, line_send, line_recv, column_send, column_recv):
+    plan = (
+        ("col", line_ref, line_got, line_send, line_recv),
+        ("row", column_ref, column_got, column_send, column_recv),
+    )
+    entry_barrier(("col", "row"))
+
+    def transfer(entry, i):
+        axis, source, target, send, recv = entry
+        me = lax.axis_index(axis)
+        other = lax.rem(me + i, lax.axis_size(axis))
+        return pltpu.make_async_remote_copy(
+            src_ref=source.at[other],
+            dst_ref=target.at[me],
+            send_sem=send.at[i],
+            recv_sem=recv.at[i],
+            device_id={axis: other},
+            device_id_type=MESH,
         )
-    return cells
+
+    keep = []
+    for entry in plan:
+        axis, source, target, send, recv = entry
+        me = lax.axis_index(axis)
+        size = lax.axis_size(axis)
+
+        def begin(i, carry, entry=entry):
+            transfer(entry, i).start()
+            return carry
+
+        lax.fori_loop(1, size, begin, 0)
+        own = pltpu.make_async_copy(source.at[me], target.at[me], own_sem.at[len(keep)])
+        own.start()
+        keep.append(own)
+    for own, entry in zip(keep, plan):
+
+        def finish(i, carry, entry=entry):
+            transfer(entry, i).wait()
+            return carry
+
+        lax.fori_loop(1, lax.axis_size(entry[0]), finish, 0)
+        own.wait()
+
+
+def swapped(lines, columns, number):
+    vmem = pl.BlockSpec(memory_space=pltpu.VMEM)
+    sems = pltpu.SemaphoreType.DMA
+    return pl.pallas_call(
+        swap_kernel,
+        out_shape=(
+            jax.ShapeDtypeStruct(lines.shape, lines.dtype),
+            jax.ShapeDtypeStruct(columns.shape, columns.dtype),
+        ),
+        in_specs=[vmem] * 2,
+        out_specs=(vmem, vmem),
+        scratch_shapes=[
+            sems((2,)),
+            sems((lines.shape[0],)),
+            sems((lines.shape[0],)),
+            sems((columns.shape[0],)),
+            sems((columns.shape[0],)),
+        ],
+        compiler_params=pltpu.CompilerParams(collective_id=number, has_side_effects=True),
+        name="swap" + str(number),
+    )(lines, columns)
+
+
+ROUND = ((-1, 0, 0), (1, 0, 1), (-1, -1, 0), (-1, 1, 0), (1, -1, 1), (1, 1, 1))
+
+
+def rim_kernel(edge_ref, side_ref, edge_got, side_got, send_sem, recv_sem):
+    height, breadth = lax.axis_size("row"), lax.axis_size("col")
+    row, col = lax.axis_index("row"), lax.axis_index("col")
+
+    def at(down, along):
+        return (lax.rem(row + down + height, height), lax.rem(col + along + breadth, breadth))
+
+    steps = [(a, b) for a, b, _ in ROUND] + [(0, -1), (0, 1)]
+    barrier = pltpu.get_barrier_semaphore()
+    for a, b in steps:
+        pl.semaphore_signal(barrier, inc=1, device_id=at(a, b), device_id_type=MESH)
+    pl.semaphore_wait(barrier, len(steps))
+    copies = []
+    for i, (a, b) in enumerate(steps):
+        edge = i < len(ROUND)
+        source = edge_ref.at[ROUND[i][2]] if edge else side_ref.at[i - len(ROUND)]
+        target = edge_got.at[i] if edge else side_got.at[i - len(ROUND)]
+        copy = pltpu.make_async_remote_copy(
+            src_ref=source,
+            dst_ref=target,
+            send_sem=send_sem.at[i],
+            recv_sem=recv_sem.at[i],
+            device_id=at(a, b),
+            device_id_type=MESH,
+        )
+        copy.start()
+        copies.append(copy)
+    for copy in copies:
+        copy.wait()
+
+
+def framed_by(cells, number):
+    rows, cols, width = cells.shape
+    edges = jnp.stack([cells[0], cells[-1]])
+    sides = jnp.stack([cells[:, 0], cells[:, -1]])
+    vmem = pl.BlockSpec(memory_space=pltpu.VMEM)
+    got, flank = pl.pallas_call(
+        rim_kernel,
+        out_shape=(
+            jax.ShapeDtypeStruct((len(ROUND), cols, width), cells.dtype),
+            jax.ShapeDtypeStruct((2, rows, width), cells.dtype),
+        ),
+        in_specs=[vmem] * 2,
+        out_specs=(vmem, vmem),
+        scratch_shapes=[pltpu.SemaphoreType.DMA((8,)), pltpu.SemaphoreType.DMA((8,))],
+        compiler_params=pltpu.CompilerParams(collective_id=number, has_side_effects=True),
+        name="rim" + str(number),
+    )(edges, sides)
+    below = jnp.concatenate([got[3][-1:], got[0], got[2][:1]])
+    above = jnp.concatenate([got[5][-1:], got[1], got[4][:1]])
+    middle = jnp.concatenate([flank[1][:, None], cells, flank[0][:, None]], 1)
+    whole = jnp.concatenate([above[None], middle, below[None]])
+    down, along = lax.axis_index("row"), lax.axis_index("col")
+    r = lax.broadcasted_iota(jnp.int32, (rows + 2, cols + 2, 1), 0)
+    c = lax.broadcasted_iota(jnp.int32, (rows + 2, cols + 2, 1), 1)
+    keep = (r > 0) | (down > 0)
+    keep = keep & ((r < rows + 1) | (down < lax.axis_size("row") - 1))
+    keep = keep & ((c > 0) | (along > 0))
+    keep = keep & ((c < cols + 1) | (along < lax.axis_size("col") - 1))
+    return jnp.where(keep, whole, jnp.zeros_like(whole))
 
 
 def layer_norm(values, gain):
@@ -175,7 +307,6 @@
 
     rates = jnp.transpose(-jnp.exp(a_log) * LOG2E, (0, 2, 1))
     place = (lax.axis_index("col") // rows) * LANES
-    empty = jnp.zeros((rank, inner), dt_weight.dtype)
     wide = []
     for pair in range(2):
         for k in range(2):
@@ -189,7 +320,7 @@
     rate_line = lax.dynamic_slice_in_dim(rates[:2], place, LANES, 2)
     rate_column = rates[2:].reshape(2, states, slices, LANES)
 
-    framed = extended(feat, (("row", 0), ("col", 1)), 1)
+    framed = framed_by(feat, 0)
     normed = layer_norm(framed, ln_gain).astype(jnp.bfloat16)
     xin = jnp.dot(
         normed.reshape(-1, width), in_weight[:, :inner], preferred_element_type=jnp.float32
@@ -212,10 +343,11 @@
     line_x = jnp.transpose(xconv.reshape(rows, cols, slices, LANES), (2, 0, 1, 3))
     line_p = jnp.broadcast_to(proj[None, :, :, : 2 * packed], (slices, rows, cols, 2 * packed))
     line_in = jnp.concatenate([line_x, line_p], -1).reshape(along, cols, 2 * LANES)
-    line_in = lax.all_to_all(line_in, "col", 0, 0, tiled=True).reshape(along * cols, 2 * LANES)
     column_in = jnp.concatenate([xconv, proj[:, :, 2 * packed :]], -1)
     column_in = jnp.swapaxes(column_in, 0, 1)
-    column_in = lax.all_to_all(column_in, "row", 0, 0, tiled=True).reshape(down * rows, -1)
+    line_in, column_in = swapped(line_in, column_in, 1)
+    line_in = line_in.reshape(along * cols, 2 * LANES)
+    column_in = column_in.reshape(down * rows, -1)
 
     line_tokens = along * cols
     line_out = pl.pallas_call(
@@ -248,11 +380,12 @@
         name="columns",
     )(column_in, scalars, wide[2:], dt_bias[2:], rate_column)
 
-    line_out = lax.all_to_all(line_out.reshape(along, cols, LANES), "col", 0, 0, tiled=True)
+    line_out, column_out = swapped(
+        line_out.reshape(along, cols, LANES), column_out.reshape(down, rows, inner), 2
+    )
     line_out = jnp.transpose(line_out.reshape(slices, rows, cols, LANES), (1, 2, 0, 3)).reshape(
         rows, cols, inner
     )
-    column_out = lax.all_to_all(column_out.reshape(down, rows, inner), "row", 0, 0, tiled=True)
     column_out = jnp.swapaxes(column_out, 0, 1)
 
     total = line_out.astype(jnp.float32) + column_out.astype(jnp.float32)
@@ -265,7 +398,7 @@
         gated.reshape(rows * cols, inner), out_weight, preferred_element_type=jnp.float32
     ).reshape(rows, cols, width)
     block = (feat.astype(jnp.float32) + projected).astype(jnp.bfloat16)
-    border = extended(block, (("row", 0), ("col", 1)), 1)
+    border = framed_by(block, 3)
     patches = jnp.concatenate(
         [border[i : i + rows, j : j + cols] for i in range(3) for j in range(3)], axis=-1
     ).reshape(rows * cols, 9 * width)

time: 126 us -> 117 us (0.929)
  the two profiles are of different devices: /device:TPU:72 before, /device:TPU:1 now
where the time goes in v1:
time: 117 us; the launch traced here: 116 us
  Pallas kernels  82.8 us (71%)
  local copies, waits for them, and re-layouts  18 us (15%)
  other arithmetic  9.76 us (8%)
  matrix products  3.84 us (3%)
  between operations  1.29 us (1%)
    pallas_call x2, Pallas kernels, swapped(): pl.pallas_call(swap_kernel, out_shape=(jax.ShapeDtypeStruct(lines.shape,...  32.7 us
    pallas_call x2, Pallas kernels, framed_by(): pl.pallas_call(rim_kernel, out_shape=(jax.ShapeDtypeStruct((len(ROUND), c...  30.8 us
    pallas_call x1, Pallas kernels, on_device(): pl.pallas_call(functools.partial(line_kernel, states), out_shape=jax.Shap...  13.6 us
    pallas_call x1, Pallas kernels, on_device(): pl.pallas_call(functools.partial(column_kernel, states), out_shape=jax.Sh...  5.75 us
    unnamed x47, local copies, waits for them, and re-layouts  3.71 us

profile of v1, /device:TPU:1, one launch (start us, length us, event | category | flops | bytes accessed | tf_op | source)
XLA Modules:
  0.0 115.7 jit_solution(13562998759388732355)
XLA Ops:
  0.9 0.7 fusion.35
  1.6 0.6 pad_maximum_fusion.4.edge_ref
  2.3 0.9 copy.73
  3.2 0.6 pad_maximum_fusion.6.side_ref
  3.8 19.5 %rim0.1 = (bf16[6,16,512]{2,1,0:T(8,128)(2,1)}, bf16[2,4,512]{2,1,0:T(4,128)(2,1)}) custom-call(bf16[2,16,512]{2,1,0:T(8,128)(2,1)} %pad_maximum_fusion.4.edge_ref, bf16[2,4,512]{2,1,0:T(4,128)(2,1)} %pad_maximum_fusion.6.side_ref), custom_call_target="tpu_custom_call" | custom-call | tf_op jit(solution)/shard_map/rim0/pallas_call | solution.py:139
  23.2 0.8 slice_bitcast_fusion.23
  24.0 0.7 slice_bitcast_fusion.7
  24.8 0.7 slice_bitcast_fusion.15
  25.5 0.2 convert_reduce_fusion
  25.8 0.2 multiply_reduce_fusion
  26.1 0.8 fusion.19
  26.9 1.5 %convolution_convert_fusion.1 = bf16[64,1024]{1,0:T(8,128)(2,1)S(1)} fusion(bf16[64,512]{1,0:T(8,128)(2,1)S(1)} %bitcast.142, bf16[512,2048]{1,0:T(8,128)(2,1)} %param.18), kind=kOutput, calls=%fused_computation.2 | convolution fusion | flops 67174400 | bytes 1245184 | tf_op jit(solution)/shard_map/dot_general | solution.py:329
  29.3 1.6 %fusion = f32[108,1024]{1,0:T(8,128)S(1)} fusion(bf16[512,2048]{1,0:T(8,128)(2,1)} %param.18, f32[512]{0:T(512)S(1)} %copy-done.14, f32[108]{0:T(128)S(1)} %rsqrt.21, f32[108]{0:T(128)S(1)} %div.30, bf16[108,512]{1,0:T(8,128)(2,1)S(1)} %concatenate.44, pred[108]{0:T(512)(128)(4,1)S(1)} %and_and_fusion.1), kind=kOutput, calls=%fused_computation.1 | convolution fusion | flops 113799168 | bytes 1604556 | tf_op jit(solution)/shard_map/dot_general | solution.py:325
  30.9 0.3 fusion.32
  31.2 0.4 copy-done.8
  31.7 1.4 %fusion.16 = bf16[4,16,1024]{2,0,1:T(4,128)(2,1)S(1)} fusion(f32[4,16,1024]{2,1,0:T(8,128)S(1)} %get-tuple-element.40, f32[4,16,1024]{2,1,0:T(8,128)S(1)} %get-tuple-element.33, f32[4,16,1024]{2,1,0:T(8,128)S(1)} %get-tuple-element.34, f32[4,16,1024]{2,1,0:T(8,128)S(1)} %get-tuple-element.35, f32[4,16,1024]{2,1,0:T(8,128)S(1)} %get-tuple-element.36, ...), kind=kLoop, calls=%fused_computation.45 | loop fusion | flops 1507328 | bytes 2531328 | tf_op jit(solution)/shard_map/convert_element_type | solution.py:338
  33.2 0.2 convolution_convert_fusion.2
  33.6 0.9 copy.94
  34.4 0.7 maximum_bitcast_fusion.column_ref
  35.2 16.5 %swap1.1 = (bf16[32,16,256]{2,1,0:T(8,128)(2,1)}, bf16[16,4,1152]{2,1,0:T(4,128)(2,1)}) custom-call(bf16[32,16,256]{2,1,0:T(8,128)(2,1)} %bitcast.129, bf16[16,4,1152]{2,1,0:T(4,128)(2,1)} %maximum_bitcast_fusion.column_ref), custom_call_target="tpu_custom_call" | custom-call | tf_op jit(solution)/shard_map/swap1/pallas_call | solution.py:80
  51.8 0.7 fusion.27.wide_ref
  52.5 0.6 fusion.37
  53.1 0.6 constant_dynamic-slice_fusion.1.bias_ref
  53.7 0.6 constant_dynamic-slice_fusion.rate_ref
  54.3 13.6 %lines.1 = bf16[512,128]{1,0:T(8,128)(2,1)} custom-call(bf16[512,256]{1,0:T(8,128)(2,1)} %bitcast.136, bf16[2,128,128]{2,1,0:T(8,128)(2,1)} %fusion.27.wide_ref, f32[2,128]{1,0:T(2,128)} %constant_dynamic-slice_fusion.1.bias_ref, f32[2,16,128]{2,1,0:T(8,128)} %constant_dynamic-slice_fusion.rate_ref), custom_call_target="tpu_custom_call" | custom-call | tf_op jit(solution)/shard_map/lines/pallas_call | solution.py:353
  68.1 0.7 copy.97.bc_ref
  68.9 0.9 pad_maximum_fusion.wide_ref
  69.7 0.7 copy.124
  70.4 5.8 %columns.1 = bf16[64,1024]{1,0:T(8,128)(2,1)} custom-call(bf16[64,1152]{1,0:T(8,128)(2,1)} %copy-done.1, f32[64,64]{1,0:T(8,128)} %copy.97.bc_ref, bf16[2,128,1024]{2,1,0:T(8,128)(2,1)} %pad_maximum_fusion.wide_ref, f32[2,1024]{1,0:T(2,128)} %get-tuple-element.80.bias_ref, f32[2,16,8,128]{3,2,1,0:T(8,128)} %bitcast.135), custom_call_target="tpu_custom_call" | custom-call | tf_op jit(solution)/shard_map/columns/pallas_call | solution.py:370
  76.1 1.6 %reshape.187.column_ref = bf16[16,4,1024]{2,1,0:T(4,128)(2,1)} reshape(bf16[64,1024]{1,0:T(8,128)(2,1)} %columns.1) | data formatting | bytes 262144 | tf_op jit(solution)/shard_map/reshape | solution.py:384
  77.8 16.2 %swap2.1 = (bf16[32,16,128]{2,1,0:T(8,128)(2,1)}, bf16[16,4,1024]{2,1,0:T(4,128)(2,1)}) custom-call(bf16[32,16,128]{2,1,0:T(8,128)(2,1)} %bitcast.131, bf16[16,4,1024]{2,1,0:T(4,128)(2,1)} %reshape.187.column_ref), custom_call_target="tpu_custom_call" | custom-call | tf_op jit(solution)/shard_map/swap2/pallas_call | solution.py:80
  93.9 1.0 copy.196
  95.0 1.1 fusion.30
  96.2 0.2 multiply_reduce_fusion.1
  96.4 0.3 fusion.17
  96.7 0.3 fusion.1
  97.2 0.6 copy.110
  98.0 0.6 copy.104.edge_ref
  98.6 0.6 pad_maximum_fusion.7.side_ref
  99.2 11.3 %rim3.1 = (bf16[6,16,512]{2,1,0:T(8,128)(2,1)}, bf16[2,4,512]{2,1,0:T(4,128)(2,1)}) custom-call(bf16[2,16,512]{2,1,0:T(8,128)(2,1)} %copy.104.edge_ref, bf16[2,4,512]{2,1,0:T(4,128)(2,1)} %pad_maximum_fusion.7.side_ref), custom_call_target="tpu_custom_call" | custom-call | tf_op jit(solution)/shard_map/rim3/pallas_call | solution.py:139
  110.5 0.8 slice_bitcast_fusion.19
  111.3 0.7 slice_bitcast_fusion.5
  112.1 0.7 slice_bitcast_fusion.13
  112.8 0.1 maximum_select_fusion
  113.7 0.2 reshape.190
  113.9 0.3 fusion.38
  114.3 0.6 broadcast_add_fusion
  115.1 0.6 copy.111
  (106 shorter events, 3.2 us)
Async XLA Ops:
  0.6 96.1 %copy-start = (bf16[1024,512]{1,0:T(8,128)(2,1)S(1)}, bf16[1024,512]{1,0:T(8,128)(2,1)}, u32[]{:S(2)}) copy-start(bf16[1024,512]{1,0:T(8,128)(2,1)} %param.27) | copy-start | bytes 3145732
  0.6 28.6 %copy-start.14 = (f32[512]{0:T(512)S(1)}, f32[512]{0:T(512)}, u32[]{:S(2)}) copy-start(f32[512]{0:T(512)} %param.17) | copy-start | bytes 6148
  30.9 0.7 copy-start.8
  30.9 0.8 copy-start.11
  31.2 2.0 %copy-start.2 = (bf16[1024,256]{1,0:T(8,128)(2,1)S(1)}, bf16[1024,256]{1,0:T(8,128)(2,1)}, u32[]{:S(2)}) copy-start(bf16[1024,256]{1,0:T(8,128)(2,1)} %param.21) | copy-start | bytes 1572868
  33.1 18.6 %copy-start.4 = (bf16[4,32,1024]{2,1,0:T(8,128)(2,1)S(1)}, bf16[4,32,1024]{2,1,0:T(8,128)(2,1)}, u32[]{:S(2)}) copy-start(bf16[4,32,1024]{2,1,0:T(8,128)(2,1)} %param.22) | copy-start | bytes 786436
  33.4 19.1 %copy-start.10 = (f32[4,1024]{1,0:T(4,128)S(1)}, f32[4,1024]{1,0:T(4,128)}, u32[]{:S(2)}) copy-start(f32[4,1024]{1,0:T(4,128)} %param.23) | copy-start | bytes 49156
  33.4 20.2 %copy-start.5 = (f32[4,1024,16]{1,2,0:T(8,128)S(1)}, f32[4,1024,16]{1,2,0:T(8,128)}, u32[]{:S(2)}) copy-start(f32[4,1024,16]{1,2,0:T(8,128)} %param.24) | copy-start | bytes 786436
  51.7 16.2 %copy-start.7 = (bf16[16,4,1152]{2,1,0:T(4,128)(2,1)S(1)}, bf16[16,4,1152]{2,1,0:T(4,128)(2,1)}, u32[]{:S(2)}) copy-start(bf16[16,4,1152]{2,1,0:T(4,128)(2,1)} %get-tuple-element.14) | copy-start | bytes 442372
  67.9 2.4 %copy-start.1 = (bf16[64,1152]{1,0:T(8,128)(2,1)}, bf16[64,1152]{1,0:T(8,128)(2,1)S(1)}, u32[]{:S(2)}) copy-start(bf16[64,1152]{1,0:T(8,128)(2,1)S(1)} %reshape.182.pack_ref) | copy-start | bytes 442372
  68.8 26.2 %copy-start.12 = (f32[1024]{0:T(1024)S(1)}, f32[1024]{0:T(1024)}, u32[]{:S(2)}) copy-start(f32[1024]{0:T(1024)} %param.25) | copy-start | bytes 12292
  69.7 26.7 %copy-start.13 = (f32[1024]{0:T(1024)S(1)}, f32[1024]{0:T(1024)}, u32[]{:S(2)}) copy-start(f32[1024]{0:T(1024)} %param.26) | copy-start | bytes 12292
  77.8 19.3 %copy-start.3 = (bf16[4,16,512]{2,1,0:T(8,128)(2,1)S(1)}, bf16[4,16,512]{2,1,0:T(8,128)(2,1)}, u32[]{:S(2)}) copy-start(bf16[4,16,512]{2,1,0:T(8,128)(2,1)} %param.16) | copy-start | bytes 196612
  97.0 16.5 %copy-start.6 = (bf16[3,3,512,16]{2,3,1,0:T(8,128)(2,1)S(1)}, bf16[3,3,512,16]{2,3,1,0:T(8,128)(2,1)}, u32[]{:S(2)}) copy-start(bf16[3,3,512,16]{2,3,1,0:T(8,128)(2,1)} %param.28) | copy-start | bytes 442372
  97.1 16.5 %copy-start.9 = (bf16[3,3,512,2]{2,3,1,0:T(2,128)(2,1)S(1)}, bf16[3,3,512,2]{2,3,1,0:T(2,128)(2,1)}, u32[]{:S(2)}) copy-start(bf16[3,3,512,2]{2,3,1,0:T(2,128)(2,1)} %param.30) | copy-start | bytes 55300
  113.0 1.3 %copy-start.15 = (f32[16]{0:T(128)S(1)}, f32[16]{0:T(128)}, u32[]{:S(2)}) copy-start(f32[16]{0:T(128)} %param.29) | copy-start | bytes 196
  113.1 1.9 %copy-start.16 = (f32[2]{0:T(128)S(1)}, f32[2]{0:T(128)}, u32[]{:S(2)}) copy-start(f32[2]{0:T(128)} %param.31) | copy-start | bytes 28

commit v2 on v1

--- a/solution.py
+++ b/solution.py
@@ -30,71 +30,49 @@
     pl.semaphore_wait(barrier, count)
 
 
-def swap_kernel(line_ref, column_ref, line_got, column_got, own_sem, line_send, line_recv, column_send, column_recv):
-    plan = (
-        ("col", line_ref, line_got, line_send, line_recv),
-        ("row", column_ref, column_got, column_send, column_recv),
-    )
-    entry_barrier(("col", "row"))
-
-    def transfer(entry, i):
-        axis, source, target, send, recv = entry
-        me = lax.axis_index(axis)
-        other = lax.rem(me + i, lax.axis_size(axis))
-        return pltpu.make_async_remote_copy(
-            src_ref=source.at[other],
-            dst_ref=target.at[me],
-            send_sem=send.at[i],
-            recv_sem=recv.at[i],
-            device_id={axis: other},
-            device_id_type=MESH,
-        )
-
-    keep = []
-    for entry in plan:
-        axis, source, target, send, recv = entry
-        me = lax.axis_index(axis)
-        size = lax.axis_size(axis)
-
-        def begin(i, carry, entry=entry):
-            transfer(entry, i).start()
-            return carry
-
-        lax.fori_loop(1, size, begin, 0)
-        own = pltpu.make_async_copy(source.at[me], target.at[me], own_sem.at[len(keep)])
-        own.start()
-        keep.append(own)
-    for own, entry in zip(keep, plan):
-
-        def finish(i, carry, entry=entry):
-            transfer(entry, i).wait()
-            return carry
-
-        lax.fori_loop(1, lax.axis_size(entry[0]), finish, 0)
-        own.wait()
-
-
-def swapped(lines, columns, number):
-    vmem = pl.BlockSpec(memory_space=pltpu.VMEM)
-    sems = pltpu.SemaphoreType.DMA
-    return pl.pallas_call(
-        swap_kernel,
-        out_shape=(
-            jax.ShapeDtypeStruct(lines.shape, lines.dtype),
-            jax.ShapeDtypeStruct(columns.shape, columns.dtype),
-        ),
-        in_specs=[vmem] * 2,
-        out_specs=(vmem, vmem),
-        scratch_shapes=[
-            sems((2,)),
-            sems((lines.shape[0],)),
-            sems((lines.shape[0],)),
-            sems((columns.shape[0],)),
-            sems((columns.shape[0],)),
-        ],
-        compiler_params=pltpu.CompilerParams(collective_id=number, has_side_effects=True),
-        name="swap" + str(number),
-    )(lines, columns)
+def transfer(axis, source, target, send, recv, i):
+    me = lax.axis_index(axis)
+    other = lax.rem(me + i, lax.axis_size(axis))
+    return pltpu.make_async_remote_copy(
+        src_ref=source.at[other],
+        dst_ref=target.at[me],
+        send_sem=send.at[i],
+        recv_sem=recv.at[i],
+        device_id={axis: other},
+        device_id_type=MESH,
+    )
+
+
+def begin(entry):
+    axis, source, target, send, recv = entry
+
+    def one(i, carry):
+        transfer(*entry, i).start()
+        return carry
+
+    lax.fori_loop(1, lax.axis_size(axis), one, 0)
+    me = lax.axis_index(axis)
+    pltpu.make_async_copy(source.at[me], target.at[me], recv.at[0]).start()
+
+
+def arrived(entry):
+    axis, source, target, send, recv = entry
+
+    def one(i, carry):
+        transfer(*entry, i).wait_recv()
+        return carry
+
+    lax.fori_loop(1, lax.axis_size(axis), one, 0)
+    me = lax.axis_index(axis)
+    pltpu.make_async_copy(source.at[me], target.at[me], recv.at[0]).wait()
+
+
+def left(entry):
+    def one(i, carry):
+        transfer(*entry, i).wait_send()
+        return carry
+
+    lax.fori_loop(1, lax.axis_size(entry[0]), one, 0)
 
 
 ROUND = ((-1, 0, 0), (1, 0, 1), (-1, -1, 0), (-1, 1, 0), (1, -1, 1), (1, 1, 1))
@@ -174,10 +152,11 @@
     return jnp.maximum(drive, 0.0) + jnp.log1p(jnp.exp(-jnp.abs(drive)))
 
 
-def line_kernel(states, pack_ref, wide_ref, bias_ref, rate_ref, out_ref, bc_ref, d_ref, u_ref, y_ref):
-    tokens = pack_ref.shape[0]
-    proj = pack_ref[:, LANES:]
-    x = pack_ref[:, :LANES].astype(jnp.float32)
+def scan_lines(states, got_ref, wide_ref, bias_ref, rate_ref, out_ref, bc_ref, d_ref, u_ref, y_ref):
+    count, depth = got_ref.shape[:2]
+    tokens = count * depth
+    proj = got_ref[:, :, LANES:].reshape(tokens, LANES)
+    x = got_ref[:, :, :LANES].reshape(tokens, LANES).astype(jnp.float32)
     for k in range(2):
         delta = step_sizes(proj, wide_ref[k], bias_ref[k : k + 1, :])
         d_ref[k] = delta
@@ -233,34 +212,40 @@
             for s in range(SUB):
                 piece = y_ref[k, pl.ds(first * SUB + s, LANES, stride=SUB), :]
                 total = piece if total is None else total + piece
-        out_ref[first : first + LANES, :] = total.astype(out_ref.dtype)
-
-
-def column_kernel(states, pack_ref, bc_ref, wide_ref, bias_ref, rate_ref, out_ref, d_ref, u_ref, y_ref):
-    tokens = pack_ref.shape[0]
-    inner = out_ref.shape[1]
-    groups = inner // LANES
-    proj = pack_ref[:, inner:]
-    for g in range(groups):
-        lanes = slice(g * LANES, (g + 1) * LANES)
-        x = pack_ref[:, lanes].astype(jnp.float32)
-        for k in range(2):
+        slots = slice(first // depth, (first + LANES) // depth)
+        out_ref[slots] = total.reshape(LANES // depth, depth, LANES).astype(out_ref.dtype)
+
+
+def scan_columns(states, x_ref, p_ref, bc_ref, wide_ref, bias_ref, rate_ref, out_ref, low_ref, d_ref, u_ref, y_ref):
+    count, depth = p_ref.shape[:2]
+    tokens = count * depth
+    groups = x_ref.shape[1] // depth
+    for q in range(count):
+        low_ref[q * depth : (q + 1) * depth, :] = p_ref[q]
+    proj = low_ref[...].astype(jnp.bfloat16)
+    x = x_ref[...].reshape(tokens * groups, LANES).astype(jnp.float32)
+    for k in range(2):
+        for g in range(groups):
+            lanes = slice(g * LANES, (g + 1) * LANES)
             delta = step_sizes(proj, wide_ref[k, :, lanes], bias_ref[k : k + 1, lanes])
             d_ref[k, pl.ds(g, tokens, stride=groups), :] = delta
-            u_ref[k, pl.ds(g, tokens, stride=groups), :] = delta * x
+        u_ref[k] = d_ref[k] * x
+    half = LANES // 2
     for k in range(2):
-
-        def step(turn, held, k=k):
+        base = k * half + half - 2 * states
+
+        def step(turn, held, k=k, base=base):
             token = turn if k == 0 else tokens - 1 - turn
             rows = pl.ds(pl.multiple_of(token * groups, groups), groups)
             d_now = d_ref[k, rows, :]
             u_now = u_ref[k, rows, :]
+            slot, part_of = token // depth, lax.rem(token, depth)
             total = None
             after = []
             for n in range(states):
                 state = jnp.exp2(d_now * rate_ref[k, n]) * held[n]
-                state = state + u_now * bc_ref[token, 2 * k * states + n]
-                part = state * bc_ref[token, (2 * k + 1) * states + n]
+                state = state + u_now * bc_ref[slot, part_of, base + n]
+                part = state * bc_ref[slot, part_of, base + states + n]
                 total = part if total is None else total + part
                 after.append(state)
             if k == 0:
@@ -271,10 +256,105 @@
 
         start = jnp.zeros((groups, LANES), jnp.float32)
         lax.fori_loop(0, tokens, step, (start,) * states, unroll=2)
-    for g in range(groups):
-        out_ref[:, g * LANES : (g + 1) * LANES] = y_ref[
-            pl.ds(g, tokens, stride=groups), :
-        ].astype(out_ref.dtype)
+    out_ref[...] = y_ref[...].reshape(out_ref.shape).astype(out_ref.dtype)
+
+
+def scan_kernel(
+    states,
+    line_ref,
+    x_ref,
+    p_ref,
+    wide_l,
+    bias_l,
+    rate_l,
+    wide_c,
+    bias_c,
+    rate_c,
+    line_back,
+    x_back,
+    line_got,
+    x_got,
+    p_got,
+    line_out,
+    x_out,
+    bc_smem,
+    bc_l,
+    d_l,
+    u_l,
+    y_l,
+    low_c,
+    d_c,
+    u_c,
+    y_c,
+    smem_sem,
+    *sems,
+):
+    lines = ("col", line_ref, line_got, sems[0], sems[1])
+    xs = ("row", x_ref, x_got, sems[2], sems[3])
+    ps = ("row", p_ref, p_got, sems[4], sems[5])
+    lines_home = ("col", line_out, line_back, sems[6], sems[7])
+    xs_home = ("row", x_out, x_back, sems[8], sems[9])
+    entry_barrier(("col", "row"))
+    begin(ps)
+    begin(xs)
+    begin(lines)
+    arrived(ps)
+    to_smem = pltpu.make_async_copy(p_got, bc_smem, smem_sem)
+    to_smem.start()
+    arrived(xs)
+    to_smem.wait()
+    scan_columns(states, x_got, p_got, bc_smem, wide_c, bias_c, rate_c, x_out, low_c, d_c, u_c, y_c)
+    begin(xs_home)
+    arrived(lines)
+    scan_lines(states, line_got, wide_l, bias_l, rate_l, line_out, bc_l, d_l, u_l, y_l)
+    begin(lines_home)
+    left(ps)
+    left(xs)
+    left(lines)
+    arrived(xs_home)
+    arrived(lines_home)
+    left(xs_home)
+    left(lines_home)
+
+
+def scanned(states, line_in, x_in, p_in, line_weights, column_weights):
+    vmem = pl.BlockSpec(memory_space=pltpu.VMEM)
+    sems = pltpu.SemaphoreType.DMA
+    f32 = jnp.float32
+    along, depth = line_in.shape[:2]
+    down, rows = p_in.shape[:2]
+    tokens = along * depth
+    packed = x_in.shape[0] * x_in.shape[1]
+    home = (along, depth, LANES)
+    return pl.pallas_call(
+        functools.partial(scan_kernel, states),
+        out_shape=(
+            jax.ShapeDtypeStruct(home, line_in.dtype),
+            jax.ShapeDtypeStruct(x_in.shape, x_in.dtype),
+        ),
+        in_specs=[vmem] * 9,
+        out_specs=(vmem, vmem),
+        scratch_shapes=[
+            pltpu.VMEM(line_in.shape, line_in.dtype),
+            pltpu.VMEM(x_in.shape, x_in.dtype),
+            pltpu.VMEM(p_in.shape, p_in.dtype),
+            pltpu.VMEM(home, line_in.dtype),
+            pltpu.VMEM(x_in.shape, x_in.dtype),
+            pltpu.SMEM(p_in.shape, p_in.dtype),
+            pltpu.VMEM((LANES, tokens), f32),
+            pltpu.VMEM((2, tokens, LANES), f32),
+            pltpu.VMEM((2, tokens, LANES), f32),
+            pltpu.VMEM((2, tokens * SUB, LANES), f32),
+            pltpu.VMEM((down * rows, LANES), f32),
+            pltpu.VMEM((2, packed, LANES), f32),
+            pltpu.VMEM((2, packed, LANES), f32),
+            pltpu.VMEM((packed, LANES), f32),
+            sems(()),
+        ]
+        + [sems((n,)) for n in (along, along, down, down, down, down, along, along, down, down)],
+        compiler_params=pltpu.CompilerParams(collective_id=1, has_side_effects=True),
+        name="scans",
+    )(line_in, x_in, p_in, *line_weights, *column_weights)
 
 
 def on_device(
@@ -303,7 +383,6 @@
     slices = inner // LANES
     down = lax.axis_size("row")
     along = lax.axis_size("col")
-    vmem = pl.BlockSpec(memory_space=pltpu.VMEM)
 
     rates = jnp.transpose(-jnp.exp(a_log) * LOG2E, (0, 2, 1))
     place = (lax.axis_index("col") // rows) * LANES
@@ -338,55 +417,29 @@
     xconv = jax.nn.silu(mixed + conv_bias).astype(jnp.bfloat16)
     proj = jnp.dot(
         xconv.reshape(rows * cols, inner), xproj_weight, preferred_element_type=jnp.float32
-    ).astype(jnp.bfloat16).reshape(rows, cols, 4 * packed)
+    ).reshape(rows, cols, 4 * packed)
 
     line_x = jnp.transpose(xconv.reshape(rows, cols, slices, LANES), (2, 0, 1, 3))
-    line_p = jnp.broadcast_to(proj[None, :, :, : 2 * packed], (slices, rows, cols, 2 * packed))
+    line_p = proj[None, :, :, : 2 * packed].astype(jnp.bfloat16)
+    line_p = jnp.broadcast_to(line_p, (slices, rows, cols, 2 * packed))
     line_in = jnp.concatenate([line_x, line_p], -1).reshape(along, cols, 2 * LANES)
-    column_in = jnp.concatenate([xconv, proj[:, :, 2 * packed :]], -1)
-    column_in = jnp.swapaxes(column_in, 0, 1)
-    line_in, column_in = swapped(line_in, column_in, 1)
-    line_in = line_in.reshape(along * cols, 2 * LANES)
-    column_in = column_in.reshape(down * rows, -1)
-
-    line_tokens = along * cols
-    line_out = pl.pallas_call(
-        functools.partial(line_kernel, states),
-        out_shape=jax.ShapeDtypeStruct((line_tokens, LANES), jnp.bfloat16),
-        in_specs=[vmem] * 4,
-        out_specs=vmem,
-        scratch_shapes=[
-            pltpu.VMEM((LANES, line_tokens), jnp.float32),
-            pltpu.VMEM((2, line_tokens, LANES), jnp.float32),
-            pltpu.VMEM((2, line_tokens, LANES), jnp.float32),
-            pltpu.VMEM((2, line_tokens * SUB, LANES), jnp.float32),
-        ],
-        name="lines",
-    )(line_in, wide_line, bias_line, rate_line)
-
-    column_tokens = down * rows
-    own = column_in[:, inner:].astype(jnp.float32).reshape(column_tokens, 2, packed)
-    scalars = own[:, :, rank:].reshape(column_tokens, 4 * states)
-    column_out = pl.pallas_call(
-        functools.partial(column_kernel, states),
-        out_shape=jax.ShapeDtypeStruct((column_tokens, inner), jnp.bfloat16),
-        in_specs=[vmem, pl.BlockSpec(memory_space=pltpu.SMEM), vmem, vmem, vmem],
-        out_specs=vmem,
-        scratch_shapes=[
-            pltpu.VMEM((2, column_tokens * slices, LANES), jnp.float32),
-            pltpu.VMEM((2, column_tokens * slices, LANES), jnp.float32),
-            pltpu.VMEM((column_tokens * slices, LANES), jnp.float32),
-        ],
-        name="columns",
-    )(column_in, scalars, wide[2:], dt_bias[2:], rate_column)
-
-    line_out, column_out = swapped(
-        line_out.reshape(along, cols, LANES), column_out.reshape(down, rows, inner), 2
+    x_in = jnp.transpose(xconv.reshape(rows, cols, slices, LANES), (1, 0, 2, 3))
+    x_in = x_in.reshape(down, rows * slices, LANES)
+    p_in = jnp.swapaxes(proj[:, :, 2 * packed :], 0, 1)
+    line_out, column_out = scanned(
+        states,
+        line_in,
+        x_in,
+        p_in,
+        (wide_line, bias_line, rate_line),
+        (wide[2:], dt_bias[2:], rate_column),
     )
     line_out = jnp.transpose(line_out.reshape(slices, rows, cols, LANES), (1, 2, 0, 3)).reshape(
         rows, cols, inner
     )
-    column_out = jnp.swapaxes(column_out, 0, 1)
+    column_out = jnp.transpose(column_out.reshape(cols, rows, slices, LANES), (1, 0, 2, 3)).reshape(
+        rows, cols, inner
+    )
 
     total = line_out.astype(jnp.float32) + column_out.astype(jnp.float32)
     total = total + dskip * xconv.astype(jnp.float32)

time: 117 us -> 102 us (0.87)
  Pallas kernels: 82.8 us -> 70.3 us
  local copies, waits for them, and re-layouts: 18 us -> 14.9 us
    pallas_call x4 -> x1, Pallas kernels: 52 us -> 40.8 us  [scanned(): pl.pallas_call(functools.partial(scan_kernel, states), out_shape=(jax.Sha...]
    reshape x5 -> x1, local copies, waits for them, and re-layouts: 2.53 us -> 0.68 us  [on_device(): x_in = x_in.reshape(down, rows * slices, LANES)]
    pallas_call x2, Pallas kernels: 30.8 us -> 29.4 us  [framed_by(): pl.pallas_call(rim_kernel, out_shape=(jax.ShapeDtypeStruct((len(ROUND), c...]
    unnamed x47 -> x44, local copies, waits for them, and re-layouts: 3.71 us -> 4.56 us
where the time goes in v2:
time: 102 us; the launch traced here: 101 us
  Pallas kernels  70.3 us (69%)
  local copies, waits for them, and re-layouts  14.9 us (15%)
  other arithmetic  10.4 us (10%)
  matrix products  4 us (4%)
  between operations  1.17 us (1%)
    pallas_call x1, Pallas kernels, scanned(): pl.pallas_call(functools.partial(scan_kernel, states), out_shape=(jax.Sha...  40.8 us
    pallas_call x2, Pallas kernels, framed_by(): pl.pallas_call(rim_kernel, out_shape=(jax.ShapeDtypeStruct((len(ROUND), c...  29.4 us
    unnamed x44, local copies, waits for them, and re-layouts  4.56 us

profile of v2, /device:TPU:1, one launch (start us, length us, event | category | flops | bytes accessed | tf_op | source)
XLA Modules:
  0.0 100.7 jit_solution(1319240569304969289)
XLA Ops:
  0.8 0.1 copy.68
  0.9 0.7 fusion.42
  1.6 0.6 pad_maximum_fusion.4.edge_ref
  2.3 0.9 copy.61
  3.2 0.6 pad_maximum_fusion.6.side_ref
  3.8 19.5 %rim0.1 = (bf16[6,16,512]{2,1,0:T(8,128)(2,1)}, bf16[2,4,512]{2,1,0:T(4,128)(2,1)}) custom-call(bf16[2,16,512]{2,1,0:T(8,128)(2,1)} %pad_maximum_fusion.4.edge_ref, bf16[2,4,512]{2,1,0:T(4,128)(2,1)} %pad_maximum_fusion.6.side_ref), custom_call_target="tpu_custom_call" | custom-call | tf_op jit(solution)/shard_map/rim0/pallas_call | solution.py:117
  23.2 0.8 slice_bitcast_fusion.23
  24.0 0.7 slice_bitcast_fusion.7
  24.8 0.7 slice_bitcast_fusion.15
  25.5 0.2 convert_reduce_fusion
  25.8 0.2 multiply_reduce_fusion
  26.1 0.8 fusion.24
  26.9 1.5 %convolution_convert_fusion.1 = bf16[64,1024]{1,0:T(8,128)(2,1)S(1)} fusion(bf16[64,512]{1,0:T(8,128)(2,1)S(1)} %bitcast.185, bf16[512,2048]{1,0:T(8,128)(2,1)} %param.18), kind=kOutput, calls=%fused_computation.2 | convolution fusion | flops 67174400 | bytes 1245184 | tf_op jit(solution)/shard_map/dot_general | solution.py:408
  29.2 1.6 %fusion = f32[108,1024]{1,0:T(8,128)S(1)} fusion(bf16[512,2048]{1,0:T(8,128)(2,1)} %param.18, f32[512]{0:T(512)S(1)} %copy-done.11, f32[108]{0:T(128)S(1)} %rsqrt.21, f32[108]{0:T(128)S(1)} %div.30, bf16[108,512]{1,0:T(8,128)(2,1)S(1)} %concatenate.41, pred[108]{0:T(512)(128)(4,1)S(1)} %and_and_fusion.1), kind=kOutput, calls=%fused_computation.1 | convolution fusion | flops 113799168 | bytes 1604556 | tf_op jit(solution)/shard_map/dot_general | solution.py:404
  31.0 0.3 multiply_convert_fusion
  31.2 0.6 copy-done.1
  31.9 0.2 fusion.5
  32.1 0.4 bitcast_bitcast_fusion
  32.5 0.7 pad_maximum_fusion.1
  33.3 0.7 copy_bitcast_fusion.x_ref
  34.0 0.6 copy.108
  34.7 0.7 fusion.35.wide_l
  35.3 0.6 fusion.43
  35.9 0.6 constant_dynamic-slice_fusion.1.bias_l
  36.6 0.6 constant_dynamic-slice_fusion.rate_l
  37.3 0.8 pad_maximum_fusion.wide_c
  38.1 0.7 copy.91
  38.8 40.8 %scans.1 = (bf16[32,16,128]{2,1,0:T(8,128)(2,1)}, bf16[16,32,128]{2,1,0:T(8,128)(2,1)}) custom-call(bf16[32,16,256]{2,1,0:T(8,128)(2,1)} %bitcast.142, bf16[16,32,128]{2,1,0:T(8,128)(2,1)} %copy_bitcast_fusion.x_ref, f32[16,4,128]{2,1,0:T(4,128)} %bitcast.147, bf16[2,128,128]{2,1,0:T(8,128)(2,1)} %fusion.35.wide_l, ...), custom_call_target="tpu_custom_call" | custom-call | tf_op jit(solution)/shard_map/scans/pallas_call | solution.py:329
  79.6 0.9 convert.20
  80.6 1.1 %fusion.20 = f32[4,16,8,128]{3,2,0,1:T(8,128)S(1)} fusion(f32[8,4,16,128]{3,2,1,0:T(8,128)S(1)} %convert.20, bf16[16,32,128]{2,1,0:T(8,128)(2,1)} %get-tuple-element.12), kind=kLoop, calls=%fused_computation.41 | loop fusion | flops 131072 | bytes 655360 | tf_op jit(solution)/shard_map/add | solution.py:444
  81.8 0.5 fusion.37
  82.3 0.6 multiply_reduce_fusion.1
  82.9 0.4 fusion.1
  83.4 0.1 fusion.25
  83.5 0.6 copy.84
  84.3 0.6 copy.78.edge_ref
  84.9 0.6 pad_maximum_fusion.7.side_ref
  85.5 10.0 %rim3.1 = (bf16[6,16,512]{2,1,0:T(8,128)(2,1)}, bf16[2,4,512]{2,1,0:T(4,128)(2,1)}) custom-call(bf16[2,16,512]{2,1,0:T(8,128)(2,1)} %copy.78.edge_ref, bf16[2,4,512]{2,1,0:T(4,128)(2,1)} %pad_maximum_fusion.7.side_ref), custom_call_target="tpu_custom_call" | custom-call | tf_op jit(solution)/shard_map/rim3/pallas_call | solution.py:117
  95.5 0.8 slice_bitcast_fusion.19
  96.3 0.7 slice_bitcast_fusion.5
  97.1 0.7 slice_bitcast_fusion.13
  97.8 0.1 maximum_select_fusion
  98.4 0.1 copy.81
  98.6 0.1 copy.82
  98.7 0.2 reshape.171
  98.9 0.3 fusion.44
  99.3 0.6 broadcast_add_fusion
  100.1 0.6 copy.85
  (89 shorter events, 2.5 us)
Async XLA Ops:
  0.6 82.3 %copy-start = (bf16[1024,512]{1,0:T(8,128)(2,1)S(1)}, bf16[1024,512]{1,0:T(8,128)(2,1)}, u32[]{:S(2)}) copy-start(bf16[1024,512]{1,0:T(8,128)(2,1)} %param.27) | copy-start | bytes 3145732
  0.6 28.6 %copy-start.11 = (f32[512]{0:T(512)S(1)}, f32[512]{0:T(512)}, u32[]{:S(2)}) copy-start(f32[512]{0:T(512)} %param.17) | copy-start | bytes 6148
  26.9 4.0 %copy-start.7 = (bf16[3,3,1024]{2,1,0:T(4,128)(2,1)S(1)}, bf16[3,3,1024]{2,1,0:T(4,128)(2,1)}, u32[]{:S(2)}) copy-start(bf16[3,3,1024]{2,1,0:T(4,128)(2,1)} %param.19) | copy-start | bytes 55300
  26.9 4.1 %copy-start.6 = (f32[1024]{0:T(1024)S(1)}, f32[1024]{0:T(1024)}, u32[]{:S(2)}) copy-start(f32[1024]{0:T(1024)} %param.20) | copy-start | bytes 12292
  30.8 1.0 %copy-start.1 = (bf16[1024,256]{1,0:T(8,128)(2,1)S(1)}, bf16[1024,256]{1,0:T(8,128)(2,1)}, u32[]{:S(2)}) copy-start(bf16[1024,256]{1,0:T(8,128)(2,1)} %param.21) | copy-start | bytes 1572868
  32.1 2.5 %copy-start.3 = (bf16[4,32,1024]{2,1,0:T(8,128)(2,1)S(1)}, bf16[4,32,1024]{2,1,0:T(8,128)(2,1)}, u32[]{:S(2)}) copy-start(bf16[4,32,1024]{2,1,0:T(8,128)(2,1)} %param.22) | copy-start | bytes 786436
  32.5 2.8 %copy-start.10 = (f32[4,1024]{1,0:T(4,128)S(1)}, f32[4,1024]{1,0:T(4,128)}, u32[]{:S(2)}) copy-start(f32[4,1024]{1,0:T(4,128)} %param.23) | copy-start | bytes 49156
  32.5 4.0 %copy-start.4 = (f32[4,1024,16]{1,2,0:T(8,128)S(1)}, f32[4,1024,16]{1,2,0:T(8,128)}, u32[]{:S(2)}) copy-start(f32[4,1024,16]{1,2,0:T(8,128)} %param.24) | copy-start | bytes 786436
  37.2 44.5 %copy-start.9 = (f32[1024]{0:T(1024)S(1)}, f32[1024]{0:T(1024)}, u32[]{:S(2)}) copy-start(f32[1024]{0:T(1024)} %param.25) | copy-start | bytes 12292
  81.7 1.2 %copy-start.14 = (f32[1024]{0:T(1024)S(1)}, f32[1024]{0:T(1024)}, u32[]{:S(2)}) copy-start(f32[1024]{0:T(1024)} %param.26) | copy-start | bytes 12292
  82.3 1.1 %copy-start.2 = (bf16[4,16,512]{2,1,0:T(8,128)(2,1)S(1)}, bf16[4,16,512]{2,1,0:T(8,128)(2,1)}, u32[]{:S(2)}) copy-start(bf16[4,16,512]{2,1,0:T(8,128)(2,1)} %param.16) | copy-start | bytes 196612
  83.4 15.2 %copy-start.5 = (bf16[3,3,512,16]{2,3,1,0:T(8,128)(2,1)S(1)}, bf16[3,3,512,16]{2,3,1,0:T(8,128)(2,1)}, u32[]{:S(2)}) copy-start(bf16[3,3,512,16]{2,3,1,0:T(8,128)(2,1)} %param.28) | copy-start | bytes 442372
  83.4 15.2 %copy-start.8 = (bf16[3,3,512,2]{2,3,1,0:T(2,128)(2,1)S(1)}, bf16[3,3,512,2]{2,3,1,0:T(2,128)(2,1)}, u32[]{:S(2)}) copy-start(bf16[3,3,512,2]{2,3,1,0:T(2,128)(2,1)} %param.30) | copy-start | bytes 55300
  98.0 1.3 %copy-start.12 = (f32[16]{0:T(128)S(1)}, f32[16]{0:T(128)}, u32[]{:S(2)}) copy-start(f32[16]{0:T(128)} %param.29) | copy-start | bytes 196
  98.1 1.9 %copy-start.13 = (f32[2]{0:T(128)S(1)}, f32[2]{0:T(128)}, u32[]{:S(2)}) copy-start(f32[2]{0:T(128)} %param.31) | copy-start | bytes 28

commit v3 on v2

--- a/solution.py
+++ b/solution.py
@@ -11,23 +11,27 @@
 LOG2E = 1.4426950408889634
 LANES = 128
 SUB = 8
+STRIDE = 32
+PAD = 32
 MESH = pl.DeviceIdType.MESH
 
 
-def entry_barrier(axes):
+def greet(axes):
     barrier = pltpu.get_barrier_semaphore()
-    count = 0
     for axis in axes:
         size = lax.axis_size(axis)
 
-        def greet(i, carry, axis=axis, size=size):
+        def one(i, carry, axis=axis, size=size):
             other = lax.rem(lax.axis_index(axis) + i, size)
             pl.semaphore_signal(barrier, inc=1, device_id={axis: other}, device_id_type=MESH)
             return carry
 
-        lax.fori_loop(1, size, greet, 0)
-        count += size - 1
-    pl.semaphore_wait(barrier, count)
+        lax.fori_loop(1, size, one, 0)
+
+
+def greeted(axes):
+    count = sum(lax.axis_size(axis) - 1 for axis in axes)
+    pl.semaphore_wait(pltpu.get_barrier_semaphore(), count)
 
 
 def transfer(axis, source, target, send, recv, i):
@@ -93,7 +97,7 @@
     copies = []
     for i, (a, b) in enumerate(steps):
         edge = i < len(ROUND)
-        source = edge_ref.at[ROUND[i][2]] if edge else side_ref.at[i - len(ROUND)]
+        source = edge_ref.at[ROUND[i][2] * (edge_ref.shape[0] - 1)] if edge else side_ref.at[i - len(ROUND)]
         target = edge_got.at[i] if edge else side_got.at[i - len(ROUND)]
         copy = pltpu.make_async_remote_copy(
             src_ref=source,
@@ -109,12 +113,11 @@
         copy.wait()
 
 
-def framed_by(cells, number):
+def rim_of(cells, number):
     rows, cols, width = cells.shape
-    edges = jnp.stack([cells[0], cells[-1]])
     sides = jnp.stack([cells[:, 0], cells[:, -1]])
     vmem = pl.BlockSpec(memory_space=pltpu.VMEM)
-    got, flank = pl.pallas_call(
+    return pl.pallas_call(
         rim_kernel,
         out_shape=(
             jax.ShapeDtypeStruct((len(ROUND), cols, width), cells.dtype),
@@ -125,7 +128,12 @@
         scratch_shapes=[pltpu.SemaphoreType.DMA((8,)), pltpu.SemaphoreType.DMA((8,))],
         compiler_params=pltpu.CompilerParams(collective_id=number, has_side_effects=True),
         name="rim" + str(number),
-    )(edges, sides)
+    )(cells, sides)
+
+
+def framed_by(cells, number):
+    rows, cols, width = cells.shape
+    got, flank = rim_of(cells, number)
     below = jnp.concatenate([got[3][-1:], got[0], got[2][:1]])
     above = jnp.concatenate([got[5][-1:], got[1], got[4][:1]])
     middle = jnp.concatenate([flank[1][:, None], cells, flank[0][:, None]], 1)
@@ -158,7 +166,7 @@
     proj = got_ref[:, :, LANES:].reshape(tokens, LANES)
     x = got_ref[:, :, :LANES].reshape(tokens, LANES).astype(jnp.float32)
     for k in range(2):
-        delta = step_sizes(proj, wide_ref[k], bias_ref[k : k + 1, :])
+        delta = step_sizes(proj, wide_ref[k], bias_ref[k])
         d_ref[k] = delta
         u_ref[k] = delta * x
     bc_ref[...] = jnp.transpose(proj.astype(jnp.float32))
@@ -178,13 +186,13 @@
             held, mats = carry
             held = list(held)
             mats = list(mats)
-            for j in range(SUB):
+            for j in range(STRIDE):
                 for k in range(2):
                     if k == 0:
-                        token = places[0] + turn * SUB + j
+                        token = places[0] + turn * STRIDE + j
                         lane = j
                     else:
-                        token = places[1] + LANES - 1 - (turn * SUB + j)
+                        token = places[1] + LANES - 1 - (turn * STRIDE + j)
                         lane = LANES - 1 - j
                     d_row = d_ref[k, pl.ds(token, 1), :]
                     u_row = u_ref[k, pl.ds(token, 1), :]
@@ -196,11 +204,11 @@
                     for n in range(1, states // SUB):
                         total = total + part[n * SUB : (n + 1) * SUB]
                     y_ref[k, pl.ds(pl.multiple_of(token * SUB, SUB), SUB), :] = total
-            mats[0] = pltpu.roll(mats[0], LANES - SUB, 1)
-            mats[1] = pltpu.roll(mats[1], SUB, 1)
+            mats[0] = pltpu.roll(mats[0], LANES - STRIDE, 1)
+            mats[1] = pltpu.roll(mats[1], STRIDE, 1)
             return (tuple(held), tuple(mats))
 
-        held, _ = lax.fori_loop(0, LANES // SUB, steps, (carry, tuple(mats)))
+        held, _ = lax.fori_loop(0, LANES // STRIDE, steps, (carry, tuple(mats)))
         return held
 
     start = jnp.zeros((states, LANES), jnp.float32)
@@ -227,7 +235,7 @@
     for k in range(2):
         for g in range(groups):
             lanes = slice(g * LANES, (g + 1) * LANES)
-            delta = step_sizes(proj, wide_ref[k, :, lanes], bias_ref[k : k + 1, lanes])
+            delta = step_sizes(proj, wide_ref[k, :, lanes], bias_ref[2 + k : 3 + k, lanes])
             d_ref[k, pl.ds(g, tokens, stride=groups), :] = delta
         u_ref[k] = d_ref[k] * x
     half = LANES // 2
@@ -243,7 +251,7 @@
             total = None
             after = []
             for n in range(states):
-                state = jnp.exp2(d_now * rate_ref[k, n]) * held[n]
+                state = jnp.exp2(d_now * rate_ref[k, n * groups : (n + 1) * groups, :]) * held[n]
                 state = state + u_now * bc_ref[slot, part_of, base + n]
                 part = state * bc_ref[slot, part_of, base + states + n]
                 total = part if total is None else total + part
@@ -259,19 +267,57 @@
     out_ref[...] = y_ref[...].reshape(out_ref.shape).astype(out_ref.dtype)
 
 
-def scan_kernel(
+def frame(feat_ref, got_ref, flank_ref, out_ref):
+    rows, cols, width = feat_ref.shape
+    down, along = lax.axis_index("row"), lax.axis_index("col")
+    f32 = jnp.float32
+    north = (down > 0).astype(f32)
+    south = (down < lax.axis_size("row") - 1).astype(f32)
+    west = (along > 0).astype(f32)
+    east = (along < lax.axis_size("col") - 1).astype(f32)
+    out_ref[...] = jnp.zeros_like(out_ref)
+    for r in range(rows):
+        out_ref[r + 1, 1 : cols + 1, :] = feat_ref[r].astype(f32)
+    left_side = flank_ref[1].astype(f32) * west
+    right_side = flank_ref[0].astype(f32) * east
+    for r in range(rows):
+        out_ref[r + 1, 0:1, :] = left_side[r : r + 1]
+        out_ref[r + 1, cols + 1 : cols + 2, :] = right_side[r : r + 1]
+    for at, scale, middle, before, after in ((0, north, 1, 5, 4), (rows + 1, south, 0, 3, 2)):
+        out_ref[at, 1 : cols + 1, :] = got_ref[middle].astype(f32) * scale
+        out_ref[at, 0:1, :] = got_ref[before].astype(f32)[cols - 1 :] * (scale * west)
+        out_ref[at, cols + 1 : cols + 2, :] = got_ref[after].astype(f32)[:1] * (scale * east)
+
+
+def block_kernel(
     states,
-    line_ref,
-    x_ref,
-    p_ref,
+    feat_ref,
+    got_ref,
+    flank_ref,
+    ln_ref,
+    in_ref,
+    cw_ref,
+    cb_ref,
+    xproj_ref,
+    dtw_ref,
+    dtb_ref,
+    rates_ref,
+    line_back,
+    x_back,
+    xconv_out,
+    gate_out,
+    frame_ref,
+    xin_ref,
+    xi_ref,
+    pi_ref,
     wide_l,
     bias_l,
     rate_l,
     wide_c,
-    bias_c,
     rate_c,
-    line_back,
-    x_back,
+    line_ref,
+    x_ref,
+    p_ref,
     line_got,
     x_got,
     p_got,
@@ -289,21 +335,73 @@
     smem_sem,
     *sems,
 ):
+    rows, cols, width = feat_ref.shape
+    inner = xconv_out.shape[1]
+    slices = inner // LANES
+    rank = dtw_ref.shape[1]
+    packed = LANES // 2
+    f32, bf16 = jnp.float32, jnp.bfloat16
     lines = ("col", line_ref, line_got, sems[0], sems[1])
     xs = ("row", x_ref, x_got, sems[2], sems[3])
     ps = ("row", p_ref, p_got, sems[4], sems[5])
     lines_home = ("col", line_out, line_back, sems[6], sems[7])
     xs_home = ("row", x_out, x_back, sems[8], sems[9])
-    entry_barrier(("col", "row"))
+    greet(("col", "row"))
+
+    frame(feat_ref, got_ref, flank_ref, frame_ref)
+    normed = layer_norm(frame_ref[...].reshape((rows + 2) * PAD, width), ln_ref[...]).astype(bf16)
+    xin = jnp.dot(normed, in_ref[:, :inner], preferred_element_type=f32).astype(bf16)
+    xin_ref[...] = xin.astype(f32).reshape(xin_ref.shape)
+    taps = [cw_ref[i].astype(f32) for i in range(3)]
+    for r in range(rows):
+        mixed = cb_ref[...]
+        for i in range(3):
+            for j in range(3):
+                mixed = mixed + xin_ref[r + i, j : j + cols, :] * taps[i][j : j + 1]
+        part = jax.nn.silu(mixed)
+        xconv_out[r * cols : (r + 1) * cols, :] = part.astype(bf16)
+    xconv = xconv_out[...]
+    proj = jnp.dot(xconv, xproj_ref[...], preferred_element_type=f32)
+    low = proj[:, :LANES].astype(bf16)
+    wider = xconv.astype(f32)
+    for r in range(rows):
+        here = slice(r * cols, (r + 1) * cols)
+        for g in range(slices):
+            lanes = slice(g * LANES, (g + 1) * LANES)
+            line_ref[g * rows + r, :, :LANES] = xconv[here, lanes]
+            line_ref[g * rows + r, :, LANES:] = low[here]
+            xi_ref[pl.ds(r * slices + g, cols, stride=rows * slices), :] = wider[here, lanes]
+        pi_ref[pl.ds(r, cols, stride=rows), :] = proj[here, LANES:]
+    x_ref[...] = xi_ref[...].reshape(x_ref.shape).astype(bf16)
+    for q in range(cols):
+        p_ref[q] = pi_ref[q * rows : (q + 1) * rows, :]
+
+    place = pl.multiple_of((lax.axis_index("col") // rows) * LANES, LANES)
+    wide_l[...] = jnp.zeros_like(wide_l)
+    wide_c[...] = jnp.zeros_like(wide_c)
+    for k in range(2):
+        at = slice(k * packed, k * packed + rank)
+        wide_l[k, at, :] = dtw_ref[k, :, pl.ds(place, LANES)]
+        wide_c[k, at, :] = dtw_ref[2 + k]
+        bias_l[k] = dtb_ref[k : k + 1, pl.ds(place, LANES)]
+        rate_l[k] = rates_ref[k, :, pl.ds(place, LANES)]
+        for g in range(slices):
+            lanes = slice(g * LANES, (g + 1) * LANES)
+            rate_c[k, pl.ds(g, states, stride=slices), :] = rates_ref[2 + k, :, lanes]
+
+    greeted(("col", "row"))
     begin(ps)
     begin(xs)
     begin(lines)
+    own = layer_norm(feat_ref[...].astype(f32).reshape(rows * cols, width), ln_ref[...])
+    gate = jnp.dot(own.astype(bf16), in_ref[:, inner:], preferred_element_type=f32)
+    gate_out[...] = gate.astype(bf16)
     arrived(ps)
     to_smem = pltpu.make_async_copy(p_got, bc_smem, smem_sem)
     to_smem.start()
     arrived(xs)
     to_smem.wait()
-    scan_columns(states, x_got, p_got, bc_smem, wide_c, bias_c, rate_c, x_out, low_c, d_c, u_c, y_c)
+    scan_columns(states, x_got, p_got, bc_smem, wide_c, dtb_ref, rate_c, x_out, low_c, d_c, u_c, y_c)
     begin(xs_home)
     arrived(lines)
     scan_lines(states, line_got, wide_l, bias_l, rate_l, line_out, bc_l, d_l, u_l, y_l)
@@ -317,30 +415,46 @@
     left(lines_home)
 
 
-def scanned(states, line_in, x_in, p_in, line_weights, column_weights):
+def scanned(states, down, along, operands):
     vmem = pl.BlockSpec(memory_space=pltpu.VMEM)
     sems = pltpu.SemaphoreType.DMA
-    f32 = jnp.float32
-    along, depth = line_in.shape[:2]
-    down, rows = p_in.shape[:2]
-    tokens = along * depth
-    packed = x_in.shape[0] * x_in.shape[1]
-    home = (along, depth, LANES)
+    f32, bf16 = jnp.float32, jnp.bfloat16
+    rows, cols, width = operands[0].shape
+    inner = operands[7].shape[0]
+    slices = inner // LANES
+    tokens = along * cols
+    packed = down * rows * slices
+    line_in, home = (along, cols, 2 * LANES), (along, cols, LANES)
+    x_in, p_in = (down, rows * slices, LANES), (down, rows, LANES)
     return pl.pallas_call(
-        functools.partial(scan_kernel, states),
+        functools.partial(block_kernel, states),
         out_shape=(
-            jax.ShapeDtypeStruct(home, line_in.dtype),
-            jax.ShapeDtypeStruct(x_in.shape, x_in.dtype),
+            jax.ShapeDtypeStruct(home, bf16),
+            jax.ShapeDtypeStruct(x_in, bf16),
+            jax.ShapeDtypeStruct((rows * cols, inner), bf16),
+            jax.ShapeDtypeStruct((rows * cols, inner), bf16),
         ),
-        in_specs=[vmem] * 9,
-        out_specs=(vmem, vmem),
+        in_specs=[vmem] * len(operands),
+        out_specs=(vmem,) * 4,
         scratch_shapes=[
-            pltpu.VMEM(line_in.shape, line_in.dtype),
-            pltpu.VMEM(x_in.shape, x_in.dtype),
-            pltpu.VMEM(p_in.shape, p_in.dtype),
-            pltpu.VMEM(home, line_in.dtype),
-            pltpu.VMEM(x_in.shape, x_in.dtype),
-            pltpu.SMEM(p_in.shape, p_in.dtype),
+            pltpu.VMEM((rows + 2, PAD, width), f32),
+            pltpu.VMEM((rows + 2, PAD, inner), f32),
+            pltpu.VMEM((packed, LANES), f32),
+            pltpu.VMEM((down * rows, LANES), f32),
+            pltpu.VMEM((2, LANES, LANES), bf16),
+            pltpu.VMEM((2, 1, LANES), f32),
+            pltpu.VMEM((2, states, LANES), f32),
+            pltpu.VMEM((2, LANES, inner), bf16),
+            pltpu.VMEM((2, states * slices, LANES), f32),
+            pltpu.VMEM(line_in, bf16),
+            pltpu.VMEM(x_in, bf16),
+            pltpu.VMEM(p_in, f32),
+            pltpu.VMEM(line_in, bf16),
+            pltpu.VMEM(x_in, bf16),
+            pltpu.VMEM(p_in, f32),
+            pltpu.VMEM(home, bf16),
+            pltpu.VMEM(x_in, bf16),
+            pltpu.SMEM(p_in, f32),
             pltpu.VMEM((LANES, tokens), f32),
             pltpu.VMEM((2, tokens, LANES), f32),
             pltpu.VMEM((2, tokens, LANES), f32),
@@ -354,7 +468,7 @@
         + [sems((n,)) for n in (along, along, down, down, down, down, along, along, down, down)],
         compiler_params=pltpu.CompilerParams(collective_id=1, has_side_effects=True),
         name="scans",
-    )(line_in, x_in, p_in, *line_weights, *column_weights)
+    )(*operands)
 
 
 def on_device(
@@ -378,62 +492,31 @@
     rows, cols, width = feat.shape
     inner = conv_weight.shape[-1]
     states = a_log.shape[-1]
-    rank = dt_weight.shape[1]
-    packed = xproj_weight.shape[1] // 4
     slices = inner // LANES
     down = lax.axis_size("row")
     along = lax.axis_size("col")
 
     rates = jnp.transpose(-jnp.exp(a_log) * LOG2E, (0, 2, 1))
-    place = (lax.axis_index("col") // rows) * LANES
-    wide = []
-    for pair in range(2):
-        for k in range(2):
-            at = k * packed
-            wide.append(
-                jnp.pad(dt_weight[2 * pair + k], ((at, 2 * packed - at - rank), (0, 0)))
-            )
-    wide = jnp.stack(wide)
-    wide_line = lax.dynamic_slice_in_dim(wide[:2], place, LANES, 2)
-    bias_line = lax.dynamic_slice_in_dim(dt_bias[:2], place, LANES, 1)
-    rate_line = lax.dynamic_slice_in_dim(rates[:2], place, LANES, 2)
-    rate_column = rates[2:].reshape(2, states, slices, LANES)
-
-    framed = framed_by(feat, 0)
-    normed = layer_norm(framed, ln_gain).astype(jnp.bfloat16)
-    xin = jnp.dot(
-        normed.reshape(-1, width), in_weight[:, :inner], preferred_element_type=jnp.float32
+    got, flank = rim_of(feat, 0)
+    line_out, column_out, xconv, gate = scanned(
+        states,
+        down,
+        along,
+        (
+            feat,
+            got,
+            flank,
+            ln_gain.reshape(1, width),
+            in_weight,
+            conv_weight,
+            conv_bias.reshape(1, inner),
+            xproj_weight,
+            dt_weight,
+            dt_bias,
+            rates,
+        ),
     )
-    xin = xin.astype(jnp.bfloat16).reshape(rows + 2, cols + 2, inner).astype(jnp.float32)
-    gate = jnp.dot(
-        normed[1:-1, 1:-1].reshape(-1, width),
-        in_weight[:, inner:],
-        preferred_element_type=jnp.float32,
-    ).astype(jnp.bfloat16)
-    mixed = jnp.zeros((rows, cols, inner), jnp.float32)
-    for i in range(3):
-        for j in range(3):
-            mixed = mixed + xin[i : i + rows, j : j + cols] * conv_weight[i, j].astype(jnp.float32)
-    xconv = jax.nn.silu(mixed + conv_bias).astype(jnp.bfloat16)
-    proj = jnp.dot(
-        xconv.reshape(rows * cols, inner), xproj_weight, preferred_element_type=jnp.float32
-    ).reshape(rows, cols, 4 * packed)
-
-    line_x = jnp.transpose(xconv.reshape(rows, cols, slices, LANES), (2, 0, 1, 3))
-    line_p = proj[None, :, :, : 2 * packed].astype(jnp.bfloat16)
-    line_p = jnp.broadcast_to(line_p, (slices, rows, cols, 2 * packed))
-    line_in = jnp.concatenate([line_x, line_p], -1).reshape(along, cols, 2 * LANES)
-    x_in = jnp.transpose(xconv.reshape(rows, cols, slices, LANES), (1, 0, 2, 3))
-    x_in = x_in.reshape(down, rows * slices, LANES)
-    p_in = jnp.swapaxes(proj[:, :, 2 * packed :], 0, 1)
-    line_out, column_out = scanned(
-        states,
-        line_in,
-        x_in,
-        p_in,
-        (wide_line, bias_line, rate_line),
-        (wide[2:], dt_bias[2:], rate_column),
-    )
+    xconv = xconv.reshape(rows, cols, inner)
     line_out = jnp.transpose(line_out.reshape(slices, rows, cols, LANES), (1, 2, 0, 3)).reshape(
         rows, cols, inner
     )

time: 102 us -> 83.9 us (0.82)
  local copies, waits for them, and re-layouts: 14.9 us -> 5.79 us
  matrix products: 4 us -> 0.54 us
  other arithmetic: 10.4 us -> 7.77 us
  Pallas kernels: 70.3 us -> 68.3 us
    dot_general x3 -> x0, matrix products: 3.31 us -> none  [the longest x1 1.58 us: on_device(): jnp.dot(normed.reshape(-1, width), in_weight[:, :inner], preferred_elemen...]
    another operation x6 -> x2, other arithmetic: 3.42 us -> 1.22 us  [rim_of(): sides = jnp.stack([cells[:, 0], cells[:, -1]])]
    pallas_call x3, Pallas kernels: 70.3 us -> 68.3 us  [the longest x1 38.7 us: scanned(): pl.pallas_call(functools.partial(block_kernel, states), out_shape=(jax.Sh...]
    unnamed x44 -> x32, local copies, waits for them, and re-layouts: 4.56 us -> 2.69 us
    transpose x1, other arithmetic: 0.04 us -> 1.69 us  [on_device(): rates = jnp.transpose(-jnp.exp(a_log) * LOG2E, (0, 2, 1))]
    slice x8 -> x0, local copies, waits for them, and re-layouts: 1.5 us -> none  [the longest x2 0.79 us: framed_by(): edges = jnp.stack([cells[0], cells[-1]])]
    dynamic_slice x2 -> x0, local copies, waits for them, and re-layouts: 1.17 us -> none  [the longest x1 0.61 us: on_device(): rate_line = lax.dynamic_slice_in_dim(rates[:2], place, LANES, 2)]
    add x1 -> x0, other arithmetic: 1.06 us -> none  [on_device(): total = line_out.astype(jnp.float32) + column_out.astype(jnp.float32)]
where the time goes in v3:
time: 83.9 us; the launch traced here: 83.3 us
  Pallas kernels  68.3 us (81%)
  other arithmetic  7.77 us (9%)
  local copies, waits for them, and re-layouts  5.79 us (7%)
  between operations  0.96 us (1%)
    pallas_call x1, Pallas kernels, scanned(): pl.pallas_call(functools.partial(block_kernel, states), out_shape=(jax.Sh...  38.7 us
    pallas_call x2, Pallas kernels, rim_of(): pl.pallas_call(rim_kernel, out_shape=(jax.ShapeDtypeStruct((len(ROUND), c...  29.6 us
    unnamed x32, local copies, waits for them, and re-layouts  2.69 us
    transpose x1, other arithmetic, on_device(): rates = jnp.transpose(-jnp.exp(a_log) * LOG2E, (0, 2, 1))  1.69 us

profile of v3, /device:TPU:1, one launch (start us, length us, event | category | flops | bytes accessed | tf_op | source)
XLA Modules:
  0.0 83.3 jit_solution(10231679521344645917)
XLA Ops:
  0.6 0.0 copy-start
  0.6 1.0 %copy.29 = bf16[4,16,512]{2,0,1:T(4,128)(2,1)S(1)} copy(bf16[4,16,512]{2,1,0:T(8,128)(2,1)} %feat_ref.1) | data formatting | bytes 131072 | tf_op args[0]
  1.6 0.6 pad_maximum_fusion.1.side_ref
  2.3 19.6 %rim0.1 = (bf16[6,16,512]{2,1,0:T(8,128)(2,1)}, bf16[2,4,512]{2,1,0:T(4,128)(2,1)}) custom-call(bf16[4,16,512]{2,1,0:T(8,128)(2,1)} %feat_ref.1, bf16[2,4,512]{2,1,0:T(4,128)(2,1)} %pad_maximum_fusion.1.side_ref), custom_call_target="tpu_custom_call" | custom-call | tf_op jit(solution)/shard_map/rim0/pallas_call | solution.py:120
  21.8 1.7 %multiply_bitcast_fusion.rates_ref = f32[4,16,1024]{2,1,0:T(8,128)} fusion(f32[4,1024,16]{1,2,0:T(8,128)} %param.24), kind=kLoop, calls=%fused_computation.19 | loop fusion | flops 131072 | bytes 524288 | tf_op jit(solution)/shard_map/transpose | solution.py:499
  23.5 38.7 %scans.1 = (bf16[32,16,128]{2,1,0:T(8,128)(2,1)}, bf16[16,32,128]{2,1,0:T(8,128)(2,1)}, bf16[64,1024]{1,0:T(8,128)(2,1)}, bf16[64,1024]{1,0:T(8,128)(2,1)}) custom-call(bf16[4,16,512]{2,1,0:T(8,128)(2,1)} %feat_ref.1, bf16[6,16,512]{2,1,0:T(8,128)(2,1)} %get-tuple-element.11.got_ref, bf16[2,4,512]{2,1,0:T(4,128)(2,1)} %get-tuple-element.12.flank_ref, ...), custom_call_target="tpu_custom_call" | custom-call | tf_op jit(solution)/shard_map/scans/pallas_call | solution.py:429
  62.2 0.0 copy-start.2
  62.2 0.0 copy-start.4
  62.2 0.0 copy-start.7
  62.2 1.0 %convert_bitcast_fusion = f32[8,8,8,128]{3,1,2,0:T(8,128)S(1)} fusion(bf16[64,1024]{1,0:T(8,128)(2,1)} %get-tuple-element.15), kind=kLoop, calls=%fused_computation.4 | loop fusion | flops 65536 | bytes 393216
  63.2 0.0 copy-start.1
  63.2 0.9 %bitcast_convert_fusion.1 = f32[8,4,16,128]{3,2,1,0:T(8,128)S(1)} fusion(bf16[32,16,128]{2,1,0:T(8,128)(2,1)} %get-tuple-element.13), kind=kLoop, calls=%fused_computation.59 | loop fusion | flops 65536 | bytes 393216 | tf_op jit(solution)/shard_map/convert_element_type | solution.py:527
  64.2 0.0 copy-done.5
  64.2 1.2 %fusion.13 = (f32[4,16]{1,0:T(4,128)S(1)}, f32[4,16,8,128]{3,2,1,0:T(8,128)S(1)}) fusion(f32[8,128]{1,0:T(8,128)S(1)} %bitcast.82, f32[8,4,16,128]{3,2,1,0:T(8,128)S(1)} %bitcast_convert_fusion.1, bf16[16,32,128]{2,1,0:T(8,128)(2,1)} %get-tuple-element.14, f32[4,16,8,128]{3,2,1,0:T(8,128)S(1)} %bitcast.77), kind=kLoop, calls=%fused_computation.25 | loop fusion | flops 327616 | bytes 921856 | tf_op jit(solution)/shard_map/reduce_sum | solution.py:153
  65.4 0.5 multiply_reduce_fusion
  65.9 0.1 rsqrt.12
  66.0 0.1 div.14
  66.1 0.0 copy-done.2
  66.1 0.0 copy-done.4
  66.1 0.0 copy-done.7
  66.1 0.2 fusion.7
  66.2 0.0 copy-done
  66.3 0.0 copy-start.3
  66.3 0.0 copy-start.6
  66.3 0.3 fusion
  66.6 0.0 copy-done.1
  66.6 0.1 fusion.12
  66.7 0.6 pad_maximum_fusion.2.side_ref
  67.3 0.6 copy.41.edge_ref
  68.0 10.1 %rim3.1 = (bf16[6,16,512]{2,1,0:T(8,128)(2,1)}, bf16[2,4,512]{2,1,0:T(4,128)(2,1)}) custom-call(bf16[4,16,512]{2,1,0:T(8,128)(2,1)} %copy.41.edge_ref, bf16[2,4,512]{2,1,0:T(4,128)(2,1)} %pad_maximum_fusion.2.side_ref), custom_call_target="tpu_custom_call" | custom-call | tf_op jit(solution)/shard_map/rim3/pallas_call | solution.py:120
  78.1 0.7 slice_bitcast_fusion.1
  78.8 0.8 slice_bitcast_fusion.11
  79.7 0.7 slice_bitcast_fusion.7
  80.4 0.1 and_and_fusion
  80.5 0.1 maximum_select_fusion
  80.7 0.0 copy-start.8
  80.7 0.0 copy-start.9
  81.1 0.1 copy.38
  81.2 0.0 copy-done.3
  81.2 0.1 copy.39
  81.3 0.2 reshape.133
  81.6 0.3 fusion.14
  81.8 0.1 copy.43
  81.9 0.0 copy-done.8
  81.9 0.6 broadcast_add_fusion
  82.6 0.1 reshape.135
  82.7 0.1 broadcast_add_fusion.1
  82.7 0.6 copy.42
  (25 shorter events, 0.6 us)
Async XLA Ops:
  0.6 65.6 %copy-start = (bf16[1024,512]{1,0:T(8,128)(2,1)S(1)}, bf16[1024,512]{1,0:T(8,128)(2,1)}, u32[]{:S(2)}) copy-start(bf16[1024,512]{1,0:T(8,128)(2,1)} %param.27) | copy-start | bytes 3145732
  23.5 40.7 %copy-start.5 = (f32[1024]{0:T(1024)S(1)}, f32[1024]{0:T(1024)}, u32[]{:S(2)}) copy-start(f32[1024]{0:T(1024)} %param.25) | copy-start | bytes 12292
  62.2 3.9 %copy-start.2 = (bf16[64,1024]{1,0:T(8,128)(2,1)S(1)}, bf16[64,1024]{1,0:T(8,128)(2,1)}, u32[]{:S(2)}) copy-start(bf16[64,1024]{1,0:T(8,128)(2,1)} %get-tuple-element.15) | copy-start | bytes 393220
  62.2 3.9 %copy-start.4 = (bf16[64,1024]{1,0:T(8,128)(2,1)S(1)}, bf16[64,1024]{1,0:T(8,128)(2,1)}, u32[]{:S(2)}) copy-start(bf16[64,1024]{1,0:T(8,128)(2,1)} %get-tuple-element.16) | copy-start | bytes 393220
  62.2 3.9 %copy-start.7 = (f32[1024]{0:T(1024)S(1)}, f32[1024]{0:T(1024)}, u32[]{:S(2)}) copy-start(f32[1024]{0:T(1024)} %param.26) | copy-start | bytes 12292
  63.2 3.4 %copy-start.1 = (bf16[4,16,512]{2,1,0:T(8,128)(2,1)S(1)}, bf16[4,16,512]{2,1,0:T(8,128)(2,1)}, u32[]{:S(2)}) copy-start(bf16[4,16,512]{2,1,0:T(8,128)(2,1)} %feat_ref.1) | copy-start | bytes 196612
  66.3 14.9 %copy-start.3 = (bf16[3,3,512,16]{2,3,1,0:T(8,128)(2,1)S(1)}, bf16[3,3,512,16]{2,3,1,0:T(8,128)(2,1)}, u32[]{:S(2)}) copy-start(bf16[3,3,512,16]{2,3,1,0:T(8,128)(2,1)} %param.28) | copy-start | bytes 442372
  66.3 14.9 %copy-start.6 = (bf16[3,3,512,2]{2,3,1,0:T(2,128)(2,1)S(1)}, bf16[3,3,512,2]{2,3,1,0:T(2,128)(2,1)}, u32[]{:S(2)}) copy-start(bf16[3,3,512,2]{2,3,1,0:T(2,128)(2,1)} %param.30) | copy-start | bytes 55300
  80.7 1.3 %copy-start.8 = (f32[16]{0:T(128)S(1)}, f32[16]{0:T(128)}, u32[]{:S(2)}) copy-start(f32[16]{0:T(128)} %param.29) | copy-start | bytes 196
  80.7 1.9 %copy-start.9 = (f32[2]{0:T(128)S(1)}, f32[2]{0:T(128)}, u32[]{:S(2)}) copy-start(f32[2]{0:T(128)} %param.31) | copy-start | bytes 28

commit v4 on v3

--- a/solution.py
+++ b/solution.py
@@ -263,7 +263,7 @@
             return tuple(after)
 
         start = jnp.zeros((groups, LANES), jnp.float32)
-        lax.fori_loop(0, tokens, step, (start,) * states, unroll=2)
+        lax.fori_loop(0, tokens, step, (start,) * states, unroll=4)
     out_ref[...] = y_ref[...].reshape(out_ref.shape).astype(out_ref.dtype)
 
 
@@ -301,7 +301,7 @@
     xproj_ref,
     dtw_ref,
     dtb_ref,
-    rates_ref,
+    alog_ref,
     line_back,
     x_back,
     xconv_out,
@@ -315,6 +315,7 @@
     rate_l,
     wide_c,
     rate_c,
+    rates_ref,
     line_ref,
     x_ref,
     p_ref,
@@ -379,6 +380,8 @@
     place = pl.multiple_of((lax.axis_index("col") // rows) * LANES, LANES)
     wide_l[...] = jnp.zeros_like(wide_l)
     wide_c[...] = jnp.zeros_like(wide_c)
+    for k in range(4):
+        rates_ref[k] = jnp.transpose(-jnp.exp(alog_ref[k]) * LOG2E)
     for k in range(2):
         at = slice(k * packed, k * packed + rank)
         wide_l[k, at, :] = dtw_ref[k, :, pl.ds(place, LANES)]
@@ -446,6 +449,7 @@
             pltpu.VMEM((2, states, LANES), f32),
             pltpu.VMEM((2, LANES, inner), bf16),
             pltpu.VMEM((2, states * slices, LANES), f32),
+            pltpu.VMEM((4, states, inner), f32),
             pltpu.VMEM(line_in, bf16),
             pltpu.VMEM(x_in, bf16),
             pltpu.VMEM(p_in, f32),
@@ -496,7 +500,6 @@
     down = lax.axis_size("row")
     along = lax.axis_size("col")
 
-    rates = jnp.transpose(-jnp.exp(a_log) * LOG2E, (0, 2, 1))
     got, flank = rim_of(feat, 0)
     line_out, column_out, xconv, gate = scanned(
         states,
@@ -513,7 +516,7 @@
             xproj_weight,
             dt_weight,
             dt_bias,
-            rates,
+            a_log,
         ),
     )
     xconv = xconv.reshape(rows, cols, inner)

time: 83.9 us -> 84.7 us (level)
  local copies, waits for them, and re-layouts: 5.79 us -> 8.68 us
  other arithmetic: 7.77 us -> 6.08 us
    unnamed x32 -> x33, local copies, waits for them, and re-layouts: 2.69 us -> 5.59 us
    transpose x1 -> x0, other arithmetic: 1.69 us -> none  [on_device(): rates = jnp.transpose(-jnp.exp(a_log) * LOG2E, (0, 2, 1))]
where the time goes in v4:
time: 84.7 us; the launch traced here: 84.2 us
  Pallas kernels  67.9 us (80%)
  local copies, waits for them, and re-layouts  8.68 us (10%)
  other arithmetic  6.08 us (7%)
  between operations  0.96 us (1%)
    pallas_call x1, Pallas kernels, scanned(): pl.pallas_call(functools.partial(block_kernel, states), out_shape=(jax.Sh...  38.2 us
    pallas_call x2, Pallas kernels, rim_of(): pl.pallas_call(rim_kernel, out_shape=(jax.ShapeDtypeStruct((len(ROUND), c...  29.7 us
    unnamed x33, local copies, waits for them, and re-layouts  5.59 us

profile of v4, /device:TPU:1, one launch (start us, length us, event | category | flops | bytes accessed | tf_op | source)
XLA Modules:
  0.0 84.2 jit_solution(1484470293224020858)
XLA Ops:
  0.6 0.0 copy-start
  0.6 1.0 %copy.30 = bf16[4,16,512]{2,0,1:T(4,128)(2,1)S(1)} copy(bf16[4,16,512]{2,1,0:T(8,128)(2,1)} %feat_ref.1) | data formatting | bytes 131072 | tf_op args[0]
  1.6 0.6 pad_maximum_fusion.1.side_ref
  2.3 19.5 %rim0.1 = (bf16[6,16,512]{2,1,0:T(8,128)(2,1)}, bf16[2,4,512]{2,1,0:T(4,128)(2,1)}) custom-call(bf16[4,16,512]{2,1,0:T(8,128)(2,1)} %feat_ref.1, bf16[2,4,512]{2,1,0:T(4,128)(2,1)} %pad_maximum_fusion.1.side_ref), custom_call_target="tpu_custom_call" | custom-call | tf_op jit(solution)/shard_map/rim0/pallas_call | solution.py:120
  21.8 2.9 %copy.33.alog_ref = f32[4,1024,16]{2,1,0:T(8,128)} copy(f32[4,1024,16]{1,2,0:T(8,128)} %param.24) | data formatting | bytes 524288 | tf_op args[8]
  24.7 38.2 %scans.1 = (bf16[32,16,128]{2,1,0:T(8,128)(2,1)}, bf16[16,32,128]{2,1,0:T(8,128)(2,1)}, bf16[64,1024]{1,0:T(8,128)(2,1)}, bf16[64,1024]{1,0:T(8,128)(2,1)}) custom-call(bf16[4,16,512]{2,1,0:T(8,128)(2,1)} %feat_ref.1, bf16[6,16,512]{2,1,0:T(8,128)(2,1)} %get-tuple-element.11.got_ref, bf16[2,4,512]{2,1,0:T(4,128)(2,1)} %get-tuple-element.12.flank_ref, ...), custom_call_target="tpu_custom_call" | custom-call | tf_op jit(solution)/shard_map/scans/pallas_call | solution.py:432
  62.9 0.0 copy-start.2
  63.0 0.0 copy-start.4
  63.0 0.0 copy-start.7
  63.0 1.0 %convert_bitcast_fusion = f32[8,8,8,128]{3,1,2,0:T(8,128)S(1)} fusion(bf16[64,1024]{1,0:T(8,128)(2,1)} %get-tuple-element.15), kind=kLoop, calls=%fused_computation.4 | loop fusion | flops 65536 | bytes 393216
  63.9 0.0 copy-start.1
  64.0 0.9 %bitcast_convert_fusion.1 = f32[8,4,16,128]{3,2,1,0:T(8,128)S(1)} fusion(bf16[32,16,128]{2,1,0:T(8,128)(2,1)} %get-tuple-element.13), kind=kLoop, calls=%fused_computation.58 | loop fusion | flops 65536 | bytes 393216 | tf_op jit(solution)/shard_map/convert_element_type | solution.py:530
  64.9 0.0 copy-done.5
  65.0 1.2 %fusion.13 = (f32[4,16]{1,0:T(4,128)S(1)}, f32[4,16,8,128]{3,2,1,0:T(8,128)S(1)}) fusion(f32[8,128]{1,0:T(8,128)S(1)} %bitcast.80, f32[8,4,16,128]{3,2,1,0:T(8,128)S(1)} %bitcast_convert_fusion.1, bf16[16,32,128]{2,1,0:T(8,128)(2,1)} %get-tuple-element.14, f32[4,16,8,128]{3,2,1,0:T(8,128)S(1)} %bitcast.75), kind=kLoop, calls=%fused_computation.24 | loop fusion | flops 327616 | bytes 921856 | tf_op jit(solution)/shard_map/reduce_sum | solution.py:153
  66.2 0.5 multiply_reduce_fusion
  66.7 0.1 rsqrt.12
  66.7 0.1 div.14
  66.8 0.0 copy-done.2
  66.8 0.0 copy-done.4
  66.8 0.0 copy-done.7
  66.8 0.2 fusion.7
  67.0 0.0 copy-done
  67.0 0.0 copy-start.3
  67.0 0.0 copy-start.6
  67.1 0.3 fusion
  67.4 0.0 copy-done.1
  67.4 0.1 fusion.12
  67.5 0.6 pad_maximum_fusion.2.side_ref
  68.1 0.6 copy.43.edge_ref
  68.8 10.2 %rim3.1 = (bf16[6,16,512]{2,1,0:T(8,128)(2,1)}, bf16[2,4,512]{2,1,0:T(4,128)(2,1)}) custom-call(bf16[4,16,512]{2,1,0:T(8,128)(2,1)} %copy.43.edge_ref, bf16[2,4,512]{2,1,0:T(4,128)(2,1)} %pad_maximum_fusion.2.side_ref), custom_call_target="tpu_custom_call" | custom-call | tf_op jit(solution)/shard_map/rim3/pallas_call | solution.py:120
  78.9 0.7 slice_bitcast_fusion.1
  79.7 0.8 slice_bitcast_fusion.11
  80.5 0.7 slice_bitcast_fusion.7
  81.3 0.1 and_and_fusion
  81.3 0.1 maximum_select_fusion
  81.6 0.0 copy-start.8
  81.6 0.0 copy-start.9
  81.9 0.1 copy.40
  82.0 0.0 copy-done.3
  82.1 0.1 copy.41
  82.2 0.2 reshape.133
  82.5 0.3 fusion.14
  82.7 0.1 copy.45
  82.8 0.0 copy-done.8
  82.8 0.6 broadcast_add_fusion
  83.4 0.1 reshape.135
  83.5 0.1 broadcast_add_fusion.1
  83.6 0.6 copy.44
  (25 shorter events, 0.6 us)
Async XLA Ops:
  0.6 66.4 %copy-start = (bf16[1024,512]{1,0:T(8,128)(2,1)S(1)}, bf16[1024,512]{1,0:T(8,128)(2,1)}, u32[]{:S(2)}) copy-start(bf16[1024,512]{1,0:T(8,128)(2,1)} %param.27) | copy-start | bytes 3145732
  24.7 40.2 %copy-start.5 = (f32[1024]{0:T(1024)S(1)}, f32[1024]{0:T(1024)}, u32[]{:S(2)}) copy-start(f32[1024]{0:T(1024)} %param.25) | copy-start | bytes 12292
  62.9 3.9 %copy-start.2 = (bf16[64,1024]{1,0:T(8,128)(2,1)S(1)}, bf16[64,1024]{1,0:T(8,128)(2,1)}, u32[]{:S(2)}) copy-start(bf16[64,1024]{1,0:T(8,128)(2,1)} %get-tuple-element.15) | copy-start | bytes 393220
  63.0 3.9 %copy-start.4 = (bf16[64,1024]{1,0:T(8,128)(2,1)S(1)}, bf16[64,1024]{1,0:T(8,128)(2,1)}, u32[]{:S(2)}) copy-start(bf16[64,1024]{1,0:T(8,128)(2,1)} %get-tuple-element.16) | copy-start | bytes 393220
  63.0 3.9 %copy-start.7 = (f32[1024]{0:T(1024)S(1)}, f32[1024]{0:T(1024)}, u32[]{:S(2)}) copy-start(f32[1024]{0:T(1024)} %param.26) | copy-start | bytes 12292
  63.9 3.4 %copy-start.1 = (bf16[4,16,512]{2,1,0:T(8,128)(2,1)S(1)}, bf16[4,16,512]{2,1,0:T(8,128)(2,1)}, u32[]{:S(2)}) copy-start(bf16[4,16,512]{2,1,0:T(8,128)(2,1)} %feat_ref.1) | copy-start | bytes 196612
  67.0 15.0 %copy-start.3 = (bf16[3,3,512,16]{2,3,1,0:T(8,128)(2,1)S(1)}, bf16[3,3,512,16]{2,3,1,0:T(8,128)(2,1)}, u32[]{:S(2)}) copy-start(bf16[3,3,512,16]{2,3,1,0:T(8,128)(2,1)} %param.28) | copy-start | bytes 442372
  67.0 15.0 %copy-start.6 = (bf16[3,3,512,2]{2,3,1,0:T(2,128)(2,1)S(1)}, bf16[3,3,512,2]{2,3,1,0:T(2,128)(2,1)}, u32[]{:S(2)}) copy-start(bf16[3,3,512,2]{2,3,1,0:T(2,128)(2,1)} %param.30) | copy-start | bytes 55300
  81.6 1.3 %copy-start.8 = (f32[16]{0:T(128)S(1)}, f32[16]{0:T(128)}, u32[]{:S(2)}) copy-start(f32[16]{0:T(128)} %param.29) | copy-start | bytes 196
  81.6 1.9 %copy-start.9 = (f32[2]{0:T(128)S(1)}, f32[2]{0:T(128)}, u32[]{:S(2)}) copy-start(f32[2]{0:T(128)} %param.31) | copy-start | bytes 28
